TPU v7x, 256 devices: a whole 4x4x8 slice. The times are simulated.
256 devices in a mesh: row: 4 (over y), col: 32 (over x_lo, z, core), feat: 2 (over x_hi).
Axes of the slice: x: 4 (x_hi: 2, x_lo: 2; x = x_hi * 2 + x_lo), y: 4, z: 8, core: 2. Of those that a mesh axis runs over, the one named last changes fastest.
Arguments:
- panel_student: bfloat16 [2048, 4096], P('row', 'feat'), may hold values from -0.01171875 to 0.01171875
- panel_teacher: bfloat16 [2048, 4096], P('row', 'feat'), may hold values from -0.01171875 to 0.01171875
- tokens_student: bfloat16 [24576, 4096], P('col', 'feat'), may hold values from -0.01171875 to 0.01171875
- tokens_teacher: bfloat16 [24576, 4096], P('col', 'feat'), may hold values from -0.01171875 to 0.01171875
Outputs:
- row_loss: float32 [2048], P(('row', 'col'))
- grad_panel: bfloat16 [2048, 4096], P(('row', 'col'), 'feat')
- grad_tokens: bfloat16 [24576, 4096], P('col', 'feat')
All inputs are finite; a program needn't handle non-finite values.
Results may differ from a plain program's by a relative error of at most 0.0058.
Values may be sent and summed in bfloat16 or wider, within the bound.
No kernel may reach another device: no remote copies, remote signals or barrier semaphores. Data moves between devices by JAX's collectives and lax.ppermute only.
A program may use at most 128 MiB of HBM per device.

v0:
```python
import jax
import jax.numpy as jnp
from jax import lax
from jax.sharding import PartitionSpec as P

epsilon = 1e-06


def squares(features):
    values = features.astype(jnp.float32)
    return jnp.sum(values * values, axis=1)


def inner(left, right):
    return jnp.einsum("rd,cd->rc", left, right, preferred_element_type=jnp.float32)


def inverse(total):
    return 1.0 / jnp.sqrt(total + epsilon)


def local(panel_student, panel_teacher, tokens_student, tokens_teacher):
    student_dots, teacher_dots, sq_ps, sq_pt, sq_ts, sq_tt = lax.psum(
        (
            inner(panel_student, tokens_student),
            inner(panel_teacher, tokens_teacher),
            squares(panel_student),
            squares(panel_teacher),
            squares(tokens_student),
            squares(tokens_teacher),
        ),
        "feat",
    )
    inv_ps = inverse(sq_ps)
    inv_pt = inverse(sq_pt)
    inv_ts = inverse(sq_ts)
    inv_tt = inverse(sq_tt)
    student_gram = student_dots * inv_ps[:, None] * inv_ts[None, :]
    teacher_gram = teacher_dots * inv_pt[:, None] * inv_tt[None, :]
    mismatch = student_gram - teacher_gram
    loss_part = jnp.sum(mismatch * mismatch, axis=1)
    doubled = (2.0 * mismatch).astype(jnp.bfloat16)
    panel_unit = panel_student.astype(jnp.float32) * inv_ps[:, None]
    token_unit = tokens_student.astype(jnp.float32) * inv_ts[:, None]
    panel_half = panel_unit.astype(jnp.bfloat16)
    token_half = token_unit.astype(jnp.bfloat16)
    panel_part = jnp.dot(doubled, token_half, preferred_element_type=jnp.float32)
    panel_term, row_loss = (
        lax.psum_scatter(panel_part, "col", scatter_dimension=0, tiled=True),
        lax.psum_scatter(loss_part, "col", scatter_dimension=0, tiled=True),
    )
    token_part = jnp.einsum("rc,rd->cd", doubled, panel_half, preferred_element_type=jnp.float32)
    token_term = lax.psum(token_part, "row")
    share = panel_student.shape[0] // lax.axis_size("col")
    offset = lax.axis_index("col") * share
    unit_rows = lax.dynamic_slice_in_dim(panel_unit, offset, share, 0)
    inv_rows = lax.dynamic_slice_in_dim(inv_ps, offset, share, 0)
    along_panel, along_tokens = lax.psum(
        (jnp.sum(unit_rows * panel_term, axis=1), jnp.sum(token_unit * token_term, axis=1)), "feat"
    )
    grad_panel = ((panel_term - unit_rows * along_panel[:, None]) * inv_rows[:, None]).astype(
        jnp.bfloat16
    )
    grad_tokens = ((token_term - token_unit * along_tokens[:, None]) * inv_ts[:, None]).astype(
        jnp.bfloat16
    )
    return (row_loss, grad_panel, grad_tokens)


def solution(mesh):
    placed = (P("row", "feat"), P("row", "feat"), P("col", "feat"), P("col", "feat"))
    return jax.shard_map(
        local,
        mesh=mesh,
        in_specs=placed,
        out_specs=(P(("row", "col")), P(("row", "col"), "feat"), P("col", "feat")),
        check_vma=False,
    )
```

profile of v0, /device:TPU:8, one launch (start us, length us, event | category | flops | bytes accessed | tf_op | source)
XLA Modules:
  0.0 405.1 jit_solution(3159031561422616562)
XLA Ops:
  7.2 5.7 %fusion.17 = f32[512,768]{1,0:T(8,128)} fusion(bf16[512,2048]{1,0:T(8,128)(2,1)} %param.5, bf16[768,2048]{1,0:T(8,128)(2,1)} %param.7), kind=kOutput, calls=%fused_computation.31 | convolution fusion | flops 1610612736 | bytes 6815744 | tf_op jit(solution)/shard_map/rd,cd->rc/dot_general | solution.py:15
  12.9 3.1 fusion.16
  16.0 2.2 multiply_reduce_fusion.1
  18.3 0.5 fusion.8
  18.7 2.6 multiply_reduce_fusion
  21.3 0.7 fusion.7
  22.0 11.1 %all-reduce.2 = (f32[768]{0:T(1024)S(1)}, f32[512]{0:T(512)S(1)}, f32[768]{0:T(1024)S(1)}, f32[512]{0:T(512)S(1)}) all-reduce(f32[768]{0:T(1024)S(1)} %multiply_reduce_fusion, f32[512]{0:T(512)S(1)} %multiply_reduce_fusion.1, f32[768]{0:T(1024)S(1)} %fusion.7, f32[512]{0:T(512)S(1)} %fusion.8), channel_id=1, replica_groups=mesh['row'=4,'col'=32,'feat'=2] {'feat'}, use_global_device_ids=true, to_apply=%region_9.0 | all-reduce | flops 2560 | bytes 20480 | tf_op jit(solution)/shard_map/psum | solution.py:23
  33.1 85.0 %all-reduce.9.cloned.1.call-done = (f32[512,768]{1,0:T(8,128)}, f32[512,768]{1,0:T(8,128)}) async-done(((f32[512,768]{1,0:T(8,128)}, f32[512,768]{1,0:T(8,128)}), (f32[512,768]{1,0:T(8,128)}, f32[512,768]{1,0:T(8,128)})) %all-reduce.9.cloned.1.call-update) | async-done | bytes 3145744 | tf_op jit(solution)/shard_map/psum | solution.py:23
  118.1 2.6 multiply_reduce_fusion.2
  120.8 1.1 copy-done.4
  121.9 4.6 %fusion.12 = f32[768,2048]{1,0:T(8,128)} fusion(f32[512,768]{1,0:T(8,128)S(1)} %get-tuple-element.12, bf16[512,2048]{1,0:T(8,128)(2,1)S(1)} %copy-done.3, f32[512]{0:T(512)S(1)} %get-tuple-element.16), kind=kOutput, calls=%fused_computation.17 | convolution fusion | flops 1614544896 | bytes 9963520 | tf_op jit(solution)/shard_map/rc,rd->cd/dot_general | solution.py:52
  126.6 5.2 %fusion.9 = f32[512,2048]{1,0:T(8,128)} fusion(bf16[768,2048]{1,0:T(8,128)(2,1)S(1)} %copy-done, f32[768]{0:T(1024)S(1)} %get-tuple-element.14, f32[512,768]{1,0:T(8,128)} %copy-done.4), kind=kOutput, calls=%fused_computation.15 | convolution fusion | flops 1616117760 | bytes 8915968 | tf_op jit(solution)/shard_map/dot_general | solution.py:47
  131.9 0.6 copy-done.6
  132.5 0.6 dynamic-slice
  133.7 4.4 %convert_multiply_fusion.2 = f32[512,2048]{1,0:T(8,128)} fusion(bf16[512,2048]{1,0:T(8,128)(2,1)} %param.4, f32[512]{0:T(512)S(1)} %get-tuple-element.16), kind=kLoop, calls=%fused_computation.11 | loop fusion | flops 2097152 | bytes 6293504 | tf_op jit(solution)/shard_map/mul | solution.py:43
  138.2 55.0 %all-reduce = f32[512]{0:T(512)S(1)} all-reduce(f32[512]{0:T(512)S(1)} %get-tuple-element.11), channel_id=2, replica_groups=mesh['row'=4,'col'=32,'feat'=2] {'col'}, use_global_device_ids=true, to_apply=%region_11.0.clone | all-reduce | flops 512 | bytes 4096
  193.2 0.6 dynamic-slice.1
  193.8 63.3 %all-reduce.7.cloned.1.call-done = f32[768,2048]{1,0:T(8,128)} async-done(((f32[768,2048]{1,0:T(8,128)}), f32[768,2048]{1,0:T(8,128)}) %all-reduce.7.cloned.1.call-update) | async-done | bytes 6291472 | tf_op jit(solution)/shard_map/psum | solution.py:53
  257.1 3.7 fusion.3
  260.9 123.8 %reduce-scatter.2.cloned.1.call-done = f32[16,2048]{1,0:T(8,128)} async-done(((f32[512,2048]{1,0:T(8,128)}), f32[16,2048]{1,0:T(8,128)}) %reduce-scatter.2.cloned.1.call-update) | async-done | bytes 131088 | tf_op jit(solution)/shard_map/reduce_scatter | solution.py:49
  384.7 1.1 multiply_reduce_fusion.3
  385.8 6.5 %all-reduce.1 = (f32[16]{0:T(128)S(1)}, f32[768]{0:T(1024)S(1)}) all-reduce(f32[16]{0:T(128)S(1)} %multiply_reduce_fusion.3, f32[768]{0:T(1024)S(1)} %fusion.3), channel_id=1, replica_groups=mesh['row'=4,'col'=32,'feat'=2] {'feat'}, use_global_device_ids=true, to_apply=%region_14.0 | all-reduce | flops 784 | bytes 6272 | tf_op jit(solution)/shard_map/psum | solution.py:58
  392.3 4.7 %fusion.6 = bf16[768,2048]{1,0:T(8,128)(2,1)} fusion(f32[768,2048]{1,0:T(8,128)} %all-reduce.7.cloned.1.call-done, bf16[768,2048]{1,0:T(8,128)(2,1)S(1)} %copy-done, f32[768]{0:T(1024)S(1)} %get-tuple-element.4, f32[768]{0:T(1024)S(1)} %get-tuple-element.14), kind=kLoop, calls=%fused_computation.8 | loop fusion | flops 9437184 | bytes 12589056 | tf_op jit(solution)/shard_map/convert_element_type | solution.py:64
  397.0 1.6 multiply_convert_fusion.3
  (21 shorter events, 0.3 us)
Async XLA Ops:
  7.2 5.7 %copy-start = (bf16[768,2048]{1,0:T(8,128)(2,1)S(1)}, bf16[768,2048]{1,0:T(8,128)(2,1)}, u32[]{:S(2)}) copy-start(bf16[768,2048]{1,0:T(8,128)(2,1)} %param.6) | copy-start | bytes 9437188
  7.2 111.0 %all-reduce.9.cloned.1.call-start = ((), (), s32[]{:S(2)}) async-start(), calls=%async_computation.3 | async-start | bytes 6291456 | tf_op jit(solution)/shard_map/psum | solution.py:23
  7.2 5.7 %copy-start.1 = (bf16[512,2048]{1,0:T(8,128)(2,1)S(1)}, bf16[512,2048]{1,0:T(8,128)(2,1)}, u32[]{:S(2)}) copy-start(bf16[512,2048]{1,0:T(8,128)(2,1)} %param.4) | copy-start | bytes 6291460
  16.0 241.1 %all-reduce.7.cloned.1.call-start = ((), (), s32[]{:S(2)}) async-start(), calls=%async_computation.2 | async-start | bytes 12582912 | tf_op jit(solution)/shard_map/psum | solution.py:53
  16.0 2.2 copy-start.2
  118.1 3.8 copy-start.3
  120.8 1.1 copy-start.4
  126.5 258.1 %reduce-scatter.2.cloned.1.call-start = ((), (), s32[]{:S(2)}) async-start(), calls=%async_computation.1 | async-start | bytes 4325376 | tf_op jit(solution)/shard_map/reduce_scatter | solution.py:49
  131.8 0.7 copy-start.6
  392.3 4.7 %copy-start.5 = (f32[16,2048]{1,0:T(8,128)S(1)}, f32[16,2048]{1,0:T(8,128)}, u32[]{:S(2)}) copy-start(f32[16,2048]{1,0:T(8,128)} %reduce-scatter.2.cloned.1.call-done) | copy-start | bytes 393220
Sparse Core Ops, SparseCore 0:
  16.1 101.9 all-reduce.8
  126.7 130.4 all-reduce.6
  259.7 124.9 reduce-scatter.1
where the time goes:
time: 405 us
  waiting for transfers between devices  272 us (67%)
  blocking collectives  72.6 us (18%)
  other arithmetic  24.2 us (6%)
  matrix products  18.5 us (5%)
  between operations  14.5 us (4%)
    reduce_scatter x1, waiting for transfers between devices, local(): lax.psum_scatter(panel_part, 'col', scatter_dimension=0, tiled=True)  124 us
    psum x1, waiting for transfers between devices, local(): lax.psum((inner(panel_student, tokens_student), inner(panel_teacher, toke...  85 us
    psum x1, waiting for transfers between devices, local(): token_term = lax.psum(token_part, 'row')  63.3 us
    unnamed x1, blocking collectives  55 us
    psum x1, blocking collectives, local(): lax.psum((inner(panel_student, tokens_student), inner(panel_teacher, toke...  11.1 us
    dot_general x2, matrix products, inner(): jnp.einsum('rd,cd->rc', left, right, preferred_element_type=jnp.float32)  8.71 us
  transfers between devices with their start and end apart: 3, of which 3 were waited for; matrix products, arithmetic and copies ran while one was open for 5% of the time, Pallas kernels for 0%

commit v1 on v0

v1 whole, which is shorter than its diff:
```python
import jax
import jax.numpy as jnp
from jax import lax
from jax.experimental import pallas as pl
from jax.experimental.pallas import tpu as pltpu
from jax.sharding import PartitionSpec as P


epsilon = 1e-06
bf16, f32 = jnp.bfloat16, jnp.float32
SMEM = pl.BlockSpec(memory_space=pltpu.SMEM)


def row_shift(x, by):
    return lax.ppermute(x, "row", [(i, (i + by) % 4) for i in range(4)])


def feat_swap(x):
    return lax.ppermute(x, "feat", [(0, 1), (1, 0)])


def col_move(x, move):
    def target(c):
        a, z, k = move(c // 16, (c // 2) % 8, c % 2)
        return a * 16 + z * 2 + k

    return lax.ppermute(x, "col", [(c, target(c)) for c in range(32)])


def core_swap(x):
    return col_move(x, lambda a, z, k: (a, z, 1 - k))


def deep_shift(x, by):
    return col_move(x, lambda a, z, k: (a, (z + by) % 8, k))


def fold_lanes(x):
    return sum(x[:, i : i + 128] for i in range(0, x.shape[1], 128))


def to_row(x):
    return jnp.sum(x.T, axis=0, keepdims=True)


def column(row, copies):
    tall = jnp.broadcast_to(row, (128, row.shape[1])).T
    return jnp.concatenate([tall] * copies, axis=1)


def shape(dims, dtype):
    return jax.ShapeDtypeStruct(dims, dtype)


def gram_kernel(ps, pt, ts, tt, student, teacher, sums, squares):
    step = pl.program_id(0)

    def inner(left, right):
        return lax.dot_general(left[...], right[...], (((1,), (1,)), ((), ())), preferred_element_type=f32)

    @pl.when(step == 0)
    def _():
        student[...] = jnp.zeros_like(student)
        teacher[...] = jnp.zeros_like(teacher)
        squares[...] = jnp.zeros_like(squares)

    student[...] += inner(ts, ps)
    teacher[...] += inner(tt, pt)
    start = 0
    for ref in (ps, pt, ts, tt):
        values = ref[...].astype(f32)
        rows = slice(start, start + values.shape[0])
        squares[rows] += fold_lanes(values * values)
        start += values.shape[0]

    @pl.when(step == pl.num_programs(0) - 1)
    def _():
        sums[...] = to_row(squares[...])


def grams(ps, pt, ts, tt):
    block = 512
    strip = lambda a: pl.BlockSpec((a.shape[0], block), lambda i: (0, i))
    same = lambda *dims: pl.BlockSpec(dims, lambda i: (0, 0))
    return pl.pallas_call(
        gram_kernel,
        grid=(ps.shape[1] // block,),
        out_shape=[shape((768, 512), f32), shape((768, 512), f32), shape((1, 2560), f32)],
        in_specs=[strip(a) for a in (ps, pt, ts, tt)],
        out_specs=[same(768, 512), same(768, 512), same(1, 2560)],
        scratch_shapes=[pltpu.VMEM((2560, 128), f32)],
        name="grams",
    )(ps, pt, ts, tt)


def inverses(mine, other):
    invs = 1.0 / jnp.sqrt(mine[...] + other[...] + epsilon)
    return invs[:, :512], invs[:, 512:1024], invs[:, 1024:1792], invs[:, 1792:]


def scaled(student, teacher, mine, other):
    inv_ps, inv_pt, inv_ts, inv_tt = inverses(mine, other)
    tall = column(inv_ts, 4)
    near = student[...] * inv_ps * tall
    return near, near - teacher[...] * inv_pt * column(inv_tt, 4), inv_ps, tall


def part_kernel(student, teacher, mine, other, out):
    out[...] = scaled(student, teacher, mine, other)[1].astype(bf16)


def mismatch_kernel(student, teacher, mine, other, partner, doubled, weighted, loss, along):
    near, part, inv_ps, tall = scaled(student, teacher, mine, other)
    mismatch = part + partner[...].astype(f32)
    twice = 2.0 * mismatch
    doubled[...] = (twice * inv_ps).astype(bf16)
    weighted[...] = (twice * tall).astype(bf16)
    loss[...] = column(jnp.sum(mismatch * mismatch, axis=0, keepdims=True), 1)
    along[...] = to_row(fold_lanes(twice * near))


def split_pair(total):
    lane = lax.broadcasted_iota(jnp.int32, total.shape, total.ndim - 1)
    high = total.astype(bf16).astype(f32)
    return jnp.where(lane == 0, high, jnp.where(lane == 1, total - high, 0.0))


def panel_kernel(core, weighted, ts, loss, away, keep, work):
    product = lax.dot_general(weighted[...], ts[...], (((0,), (0,)), ((), ())), preferred_element_type=f32)
    work[:, :, :, :2048] = product.reshape(16, 2, 16, 2048)
    work[:, :, :, 2048:] = loss[...].reshape(16, 2, 16, 128)
    other = work[:, 1 - core[0]]
    away[:, :, :2048] = other[:, :, :2048].astype(bf16)
    away[:, :, 2048:] = split_pair(other[:, :, 2048:]).astype(bf16)
    own = work[:, core[0]]
    lane = lax.broadcasted_iota(jnp.int32, (16, 16, 128), 2)
    keep[:, :, :2048] = own[:, :, :2048]
    keep[:, :, 2048:] = jnp.where(lane == 0, own[:, :, 2048:], 0.0)


def join_kernel(keep, away, out):
    out[:, :, :2048] = (keep[:, :, :2048] + away[:, :, :2048].astype(f32)).astype(bf16)
    total = jnp.sum(keep[:, :, 2048:] + away[:, :, 2048:].astype(f32), axis=2, keepdims=True)
    out[:, :, 2048:] = split_pair(jnp.broadcast_to(total, (16, 16, 128))).astype(bf16)


def token_kernel(place, d0, dl, dr, do, ps, *refs):
    pieces, (ts, mine, other, along, out, work) = refs[:12], refs[12:]
    deep, core = place[0], place[1]
    for order, (a, b) in enumerate(((deep, core), (1 - deep, core), (deep, 1 - core), (1 - deep, 1 - core))):
        start = pl.multiple_of((a * 2 + b) * 128, 128)
        for side in range(3):
            work[side, pl.ds(start, 128)] = pieces[order * 3 + side][...]

    def dot(a, b):
        return jnp.dot(a, b, preferred_element_type=f32)

    total = dot(d0[...], ps[...]) + dot(dl[...], work[0]) + dot(dr[...], work[1]) + dot(do[...], work[2])
    inv_ts = inverses(mine, other)[2]
    copies = ts.shape[1] // 128
    scale = column(inv_ts, copies)
    shade = column(inv_ts * inv_ts * along[...], copies)
    out[...] = (total * scale - ts[...].astype(f32) * shade).astype(bf16)


def token_grad(place, doubled, ps, pieces, ts, mine, other, along):
    rows, width = ts.shape
    block = 512
    whole = lambda a: pl.BlockSpec(a.shape, lambda i: (0, 0))
    strip = lambda a: pl.BlockSpec((a.shape[0], block), lambda i: (0, i))
    return pl.pallas_call(
        token_kernel,
        grid=(width // block,),
        out_shape=shape((rows, width), bf16),
        in_specs=[SMEM]
        + [whole(a) for a in doubled]
        + [strip(a) for a in (ps, *pieces, ts)]
        + [whole(a) for a in (mine, other, along)],
        out_specs=pl.BlockSpec((rows, block), lambda i: (0, i)),
        scratch_shapes=[pltpu.VMEM((3, 512, block), bf16)],
        name="tokens",
    )(place, *doubled, ps, *pieces, ts, mine, other, along)


def local(panel_student, panel_teacher, tokens_student, tokens_teacher):
    col = lax.axis_index("col")
    deep, core = (col // 2) % 2, col % 2
    place = jnp.stack([deep, core]).astype(jnp.int32)

    quarter = lax.dynamic_slice_in_dim(panel_student, (deep * 2 + core) * 128, 128, 0)
    left = row_shift(quarter, 1)
    right = row_shift(quarter, 3)
    far = row_shift(quarter, 2)
    first = (left, right, far)
    second = (deep_shift(left, 1), deep_shift(right, 7), deep_shift(far, 1))
    third = tuple(core_swap(a) for a in first)
    fourth = tuple(core_swap(a) for a in second)
    pieces = first + second + third + fourth

    student, teacher, mine = grams(panel_student, panel_teacher, tokens_student, tokens_teacher)
    other = feat_swap(mine)
    part = pl.pallas_call(part_kernel, out_shape=shape((768, 512), bf16), name="part")(student, teacher, mine, other)
    partner = feat_swap(part)
    doubled, weighted, loss, along = pl.pallas_call(
        mismatch_kernel,
        out_shape=[shape((768, 512), bf16), shape((768, 512), bf16), shape((512, 128), f32), shape((1, 768), f32)],
        name="mismatch",
    )(student, teacher, mine, other, partner)
    gathered = (doubled, row_shift(doubled, 1), row_shift(doubled, 3), row_shift(doubled, 2))

    away, keep = pl.pallas_call(
        panel_kernel,
        out_shape=[shape((16, 16, 2176), bf16), shape((16, 16, 2176), f32)],
        in_specs=[SMEM] + [pl.BlockSpec(memory_space=pltpu.VMEM)] * 3,
        scratch_shapes=[pltpu.VMEM((16, 2, 16, 2176), f32)],
        name="panel",
    )(place[1:], weighted, tokens_student, loss)
    away = core_swap(away)

    along += feat_swap(along)
    along += row_shift(along, 1)
    along += row_shift(along, 2)

    joined = pl.pallas_call(join_kernel, out_shape=shape((16, 16, 2176), bf16), name="join")(keep, away)
    groups = [[a * 16 + z * 2 + k for a in range(2) for z in range(8)] for k in range(2)]
    spread = lax.all_to_all(joined, "col", 0, 0, axis_index_groups=groups, tiled=True)

    total = jnp.sum(spread.astype(f32), axis=0)
    panel_term = total[:, :2048]
    row_loss = total[:, 2048] + total[:, 2049]
    rows = lambda a: lax.dynamic_slice_in_dim(a, col * 16, 16, 0)
    inv_rows = 1.0 / jnp.sqrt(rows(mine[0]) + rows(other[0]) + epsilon)
    unit = rows(panel_student).astype(f32) * inv_rows[:, None]
    along_rows = jnp.sum(unit * panel_term, axis=1)
    along_rows += feat_swap(along_rows)
    grad_tokens = token_grad(place, gathered, panel_student, pieces, tokens_student, mine, other, along)
    grad_panel = ((panel_term - unit * along_rows[:, None]) * inv_rows[:, None]).astype(bf16)
    return (row_loss, grad_panel, grad_tokens)


def solution(mesh):
    placed = (P("row", "feat"), P("row", "feat"), P("col", "feat"), P("col", "feat"))
    return jax.shard_map(
        local,
        mesh=mesh,
        in_specs=placed,
        out_specs=(P(("row", "col")), P(("row", "col"), "feat"), P("col", "feat")),
        check_vma=False,
    )
```

time: 405 us -> 179 us (0.44)
  waiting for transfers between devices: 272 us -> 87.6 us
  blocking collectives: 72.6 us -> 0 us
  Pallas kernels: 0 us -> 40.7 us
  starting transfers between devices: 0.12 us -> 37.9 us
  other arithmetic: 24.2 us -> 5.48 us
  matrix products: 18.5 us -> 0 us
  between operations: 14.5 us -> 0.74 us
    psum x2 -> x0, waiting for transfers between devices: 148 us -> none  [the longest x1 85 us: local(): lax.psum((inner(panel_student, tokens_student), inner(panel_teacher, toke...]
    reduce_scatter x1 -> x0, waiting for transfers between devices: 124 us -> none  [local(): lax.psum_scatter(panel_part, 'col', scatter_dimension=0, tiled=True)]
    ppermute x0 -> x22, waiting for transfers between devices: none -> 87.6 us  [the longest x8 35.1 us: row_shift(): return lax.ppermute(x, 'row', [(i, (i + by) % 4) for i in range(4)])]
    unnamed x1 -> x0, blocking collectives: 55 us -> none
    pallas_call x0 -> x6, Pallas kernels: none -> 40.7 us  [the longest x1 12.2 us: grams(): pl.pallas_call(gram_kernel, grid=(ps.shape[1] // block,), out_shape=[shap...]
    ppermute x0 -> x22, starting transfers between devices: none -> 28.2 us  [the longest x4 11.8 us: feat_swap(): return lax.ppermute(x, 'feat', [(0, 1), (1, 0)])]
    dot_general x4 -> x0, matrix products: 18.5 us -> none  [the longest x2 8.71 us: inner(): jnp.einsum('rd,cd->rc', left, right, preferred_element_type=jnp.float32)]
    psum x2 -> x0, blocking collectives: 17.6 us -> none  [the longest x1 11.1 us: local(): lax.psum((inner(panel_student, tokens_student), inner(panel_teacher, toke...]
  transfers between devices with their start and end apart: 3 -> 23, of which waited for: 3 -> 12; matrix products, arithmetic and copies ran while one was open for 5% -> 2% of each run, Pallas kernels for 0% -> 9%
where the time goes in v1:
time: 179 us; the launch traced here: 177 us
  waiting for transfers between devices  87.6 us (49%)
  Pallas kernels  40.7 us (23%)
  starting transfers between devices  37.9 us (21%)
  other arithmetic  5.48 us (3%)
  local copies, waits for them, and re-layouts  5.06 us (3%)
    ppermute x8, waiting for transfers between devices, row_shift(): return lax.ppermute(x, 'row', [(i, (i + by) % 4) for i in range(4)])  35.1 us
    ppermute x10, waiting for transfers between devices, col_move(): return lax.ppermute(x, 'col', [(c, target(c)) for c in range(32)])  29.4 us
    ppermute x4, waiting for transfers between devices, feat_swap(): return lax.ppermute(x, 'feat', [(0, 1), (1, 0)])  23.2 us
    pallas_call x1, Pallas kernels, grams(): pl.pallas_call(gram_kernel, grid=(ps.shape[1] // block,), out_shape=[shap...  12.2 us
    ppermute x4, starting transfers between devices, feat_swap(): return lax.ppermute(x, 'feat', [(0, 1), (1, 0)])  11.8 us
    pallas_call x1, Pallas kernels, token_grad(): pl.pallas_call(token_kernel, grid=(width // block,), out_shape=shape((row...  11.7 us
    ppermute x8, starting transfers between devices, row_shift(): return lax.ppermute(x, 'row', [(i, (i + by) % 4) for i in range(4)])  11.3 us
    all_to_all x1, starting transfers between devices, local(): lax.all_to_all(joined, 'col', 0, 0, axis_index_groups=groups, tiled=True)  9.63 us
  transfers between devices with their start and end apart: 23, of which 12 were waited for; matrix products, arithmetic and copies ran while one was open for 2% of the time, Pallas kernels for 9%

profile of v1, /device:TPU:8, one launch (start us, length us, event | category | flops | bytes accessed | tf_op | source)
XLA Modules:
  0.0 177.4 jit_solution(7909861107896281596)
XLA Ops:
  0.6 12.2 %grams.1 = (f32[768,512]{1,0:T(8,128)}, f32[768,512]{1,0:T(8,128)}, f32[1,2560]{1,0:T(1,128)}) custom-call(bf16[512,2048]{1,0:T(8,128)(2,1)} %ps.3, bf16[512,2048]{1,0:T(8,128)(2,1)} %pt.1, bf16[768,2048]{1,0:T(8,128)(2,1)} %refs_12_.1, bf16[768,2048]{1,0:T(8,128)(2,1)} %tt.1), custom_call_target="tpu_custom_call" | custom-call | tf_op jit(solution)/shard_map/grams/pallas_call | solution.py:85
  12.8 3.0 %collective-permute-start = (f32[1,2560]{1,0:T(1,128)}, f32[1,2560]{1,0:T(1,128)S(1)}, u32[]{:S(2)}, u32[]{:S(2)}) collective-permute-start(f32[1,2560]{1,0:T(1,128)} %get-tuple-element.14.mine.refs_13_), channel_id=1, source_target_pairs={{0,1},{1,0},{2,3},{3,2},{4,5},{5,4},{6,7},{7,6},{8,9},{9,8},{10,11... | collective-permute-start | bytes 30728 | tf_op jit(solution)/shard_map/ppermute | solution.py:19
  15.9 2.4 %collective-permute-done.other.refs_14_ = f32[1,2560]{1,0:T(1,128)S(1)} collective-permute-done((f32[1,2560]{1,0:T(1,128)}, f32[1,2560]{1,0:T(1,128)S(1)}, u32[]{:S(2)}, u32[]{:S(2)}) %collective-permute-start) | collective-permute-done | bytes 10272 | tf_op jit(solution)/shard_map/ppermute | solution.py:19
  18.8 3.2 %part.1 = bf16[768,512]{1,0:T(8,128)(2,1)} custom-call(f32[768,512]{1,0:T(8,128)} %get-tuple-element.12.student, f32[768,512]{1,0:T(8,128)} %get-tuple-element.13.teacher, f32[1,2560]{1,0:T(1,128)} %get-tuple-element.14.mine.refs_13_, f32[1,2560]{1,0:T(1,128)} %copy-done.12), custom_call_target="tpu_custom_call" | custom-call | tf_op jit(solution)/shard_map/part/pallas_call | solution.py:202
  22.0 3.0 %collective-permute-start.1 = (bf16[768,512]{1,0:T(8,128)(2,1)}, bf16[768,512]{1,0:T(8,128)(2,1)S(1)}, u32[]{:S(2)}, u32[]{:S(2)}) collective-permute-start(bf16[768,512]{1,0:T(8,128)(2,1)} %part.1), channel_id=1, source_target_pairs={{0,1},{1,0},{2,3},{3,2},{4,5},{5,4},{6,7},{7,6},{8,9},{9,8},{10,11... | collective-permute-start | bytes 2359304 | tf_op jit(solution)/shard_map/ppermute | solution.py:19
  25.0 16.8 %collective-permute-done.1.partner = bf16[768,512]{1,0:T(8,128)(2,1)S(1)} collective-permute-done((bf16[768,512]{1,0:T(8,128)(2,1)}, bf16[768,512]{1,0:T(8,128)(2,1)S(1)}, u32[]{:S(2)}, u32[]{:S(2)}) %collective-permute-start.1) | collective-permute-done | bytes 786464 | tf_op jit(solution)/shard_map/ppermute | solution.py:19
  42.8 4.4 %mismatch.1 = (bf16[768,512]{1,0:T(8,128)(2,1)}, bf16[768,512]{1,0:T(8,128)(2,1)}, f32[512,128]{1,0:T(8,128)}, f32[1,768]{1,0:T(1,128)}) custom-call(f32[768,512]{1,0:T(8,128)} %get-tuple-element.12.student, f32[768,512]{1,0:T(8,128)} %get-tuple-element.13.teacher, f32[1,2560]{1,0:T(1,128)} %get-tuple-element.14.mine.refs_13_, f32[1,2560]{1,0:T(1,128)} %copy-done.12, ...), custom_call_target="tpu_custom_call" | custom-call | tf_op jit(solution)/shard_map/mismatch/pallas_call | solution.py:204
  47.1 5.8 %panel.1 = (bf16[16,16,2176]{2,1,0:T(8,128)(2,1)}, f32[16,16,2176]{2,1,0:T(8,128)}) custom-call(s32[1]{0:T(128)} %bitcast.core, bf16[768,512]{1,0:T(8,128)(2,1)} %get-tuple-element.15.weighted, bf16[768,2048]{1,0:T(8,128)(2,1)} %refs_12_.1, f32[512,128]{1,0:T(8,128)} %get-tuple-element.16.loss), custom_call_target="tpu_custom_call" | custom-call | tf_op jit(solution)/shard_map/panel/pallas_call | solution.py:211
  54.0 1.7 collective-permute-start.7
  57.1 3.4 %join.1 = bf16[16,16,2176]{2,1,0:T(8,128)(2,1)} custom-call(f32[16,16,2176]{2,1,0:T(8,128)} %get-tuple-element.17.keep, bf16[16,16,2176]{2,1,0:T(8,128)(2,1)} %copy-done), custom_call_target="tpu_custom_call" | custom-call | tf_op jit(solution)/shard_map/join/pallas_call | solution.py:224
  60.5 9.6 %all-to-all-start = ((bf16[16,16,2176]{2,1,0:T(8,128)(2,1)}), bf16[16,16,2176]{2,1,0:T(8,128)(2,1)S(1)}, u32[]{:S(2)}, u32[]{:S(2)}) async-start(bf16[16,16,2176]{2,1,0:T(8,128)(2,1)} %join.1), calls=%async_computation | async-start | bytes 2228224 | tf_op jit(solution)/shard_map/all_to_all | solution.py:226
  70.1 2.4 %collective-permute-start.9 = (bf16[128,2048]{1,0:T(8,128)(2,1)S(1)}, bf16[128,2048]{1,0:T(8,128)(2,1)S(1)}, u32[]{:S(2)}, u32[]{:S(2)}) collective-permute-start(bf16[128,2048]{1,0:T(8,128)(2,1)S(1)} %constant_dynamic-slice_fusion), channel_id=1, source_target_pairs={{0,128},{64,192},{128,0},{192,64},{1,129},{65,193},{129,1},{193,65... | collective-permute-start | bytes 1572872 | tf_op jit(solution)/shard_map/ppermute | solution.py:15
  72.5 1.8 %collective-permute-start.10 = (bf16[128,2048]{1,0:T(8,128)(2,1)S(1)}, bf16[128,2048]{1,0:T(8,128)(2,1)S(1)}, u32[]{:S(2)}, u32[]{:S(2)}) collective-permute-start(bf16[128,2048]{1,0:T(8,128)(2,1)S(1)} %collective-permute-done.7.refs_0_), channel_id=1, source_target_pairs={{0,4},{2,6},{4,8},{6,10},{8,12},{10,14},{12,16},{14,18},{16,20},{1... | collective-permute-start | bytes 1572872 | tf_op jit(solution)/shard_map/ppermute | solution.py:27
  75.8 2.9 %collective-permute-start.19 = (f32[1,768]{1,0:T(1,128)S(1)}, f32[1,768]{1,0:T(1,128)S(1)}, u32[]{:S(2)}, u32[]{:S(2)}) collective-permute-start(f32[1,768]{1,0:T(1,128)S(1)} %copy-done.13), channel_id=1, source_target_pairs={{0,1},{1,0},{2,3},{3,2},{4,5},{5,4},{6,7},{7,6},{8,9},{9,8},{10,11... | collective-permute-start | bytes 9224 | tf_op jit(solution)/shard_map/ppermute | solution.py:19
  78.7 2.4 %collective-permute-done.19 = f32[1,768]{1,0:T(1,128)S(1)} collective-permute-done((f32[1,768]{1,0:T(1,128)S(1)}, f32[1,768]{1,0:T(1,128)S(1)}, u32[]{:S(2)}, u32[]{:S(2)}) %collective-permute-start.19) | collective-permute-done | bytes 3104 | tf_op jit(solution)/shard_map/ppermute | solution.py:19
  82.1 3.3 %collective-permute-done.20 = f32[1,768]{1,0:T(1,128)S(1)} collective-permute-done((f32[1,768]{1,0:T(1,128)S(1)}, f32[1,768]{1,0:T(1,128)S(1)}, u32[]{:S(2)}, u32[]{:S(2)}) %collective-permute-start.20) | collective-permute-done | bytes 3104 | tf_op jit(solution)/shard_map/ppermute | solution.py:15
  88.1 2.4 %collective-permute-done.21 = f32[1,768]{1,0:T(1,128)S(1)} collective-permute-done((f32[1,768]{1,0:T(1,128)S(1)}, f32[1,768]{1,0:T(1,128)S(1)}, u32[]{:S(2)}, u32[]{:S(2)}) %collective-permute-start.21) | collective-permute-done | bytes 3104 | tf_op jit(solution)/shard_map/ppermute | solution.py:15
  90.5 19.3 %collective-permute-done.10.refs_3_ = bf16[128,2048]{1,0:T(8,128)(2,1)S(1)} collective-permute-done((bf16[128,2048]{1,0:T(8,128)(2,1)S(1)}, bf16[128,2048]{1,0:T(8,128)(2,1)S(1)}, u32[]{:S(2)}, u32[]{:S(2)}) %collective-permute-start.10) | collective-permute-done | bytes 524320 | tf_op jit(solution)/shard_map/ppermute | solution.py:27
  110.3 9.8 %collective-permute-done.12.refs_5_ = bf16[128,2048]{1,0:T(8,128)(2,1)} collective-permute-done((bf16[128,2048]{1,0:T(8,128)(2,1)S(1)}, bf16[128,2048]{1,0:T(8,128)(2,1)}, u32[]{:S(2)}, u32[]{:S(2)}) %collective-permute-start.12) | collective-permute-done | bytes 524320 | tf_op jit(solution)/shard_map/ppermute | solution.py:27
  122.3 2.3 %collective-permute-start.6 = (bf16[768,512]{1,0:T(8,128)(2,1)S(1)}, bf16[768,512]{1,0:T(8,128)(2,1)}, u32[]{:S(2)}, u32[]{:S(2)}) collective-permute-start(bf16[768,512]{1,0:T(8,128)(2,1)S(1)} %copy-done.1), channel_id=1, source_target_pairs={{0,128},{64,192},{128,0},{192,64},{1,129},{65,193},{129,1},{193,65... | collective-permute-start | bytes 2359304 | tf_op jit(solution)/shard_map/ppermute | solution.py:15
  128.5 12.1 %collective-permute-done.4.dl = bf16[768,512]{1,0:T(8,128)(2,1)S(1)} collective-permute-done((bf16[768,512]{1,0:T(8,128)(2,1)S(1)}, bf16[768,512]{1,0:T(8,128)(2,1)S(1)}, u32[]{:S(2)}, u32[]{:S(2)}) %collective-permute-start.4) | collective-permute-done | bytes 786464 | tf_op jit(solution)/shard_map/ppermute | solution.py:15
  141.5 16.3 %collective-permute-done.6.do = bf16[768,512]{1,0:T(8,128)(2,1)} collective-permute-done((bf16[768,512]{1,0:T(8,128)(2,1)S(1)}, bf16[768,512]{1,0:T(8,128)(2,1)}, u32[]{:S(2)}, u32[]{:S(2)}) %collective-permute-start.6) | collective-permute-done | bytes 786464 | tf_op jit(solution)/shard_map/ppermute | solution.py:15
  157.8 11.7 %tokens.1 = bf16[768,2048]{1,0:T(8,128)(2,1)} custom-call(s32[2]{0:T(128)} %pad_add_fusion.place, bf16[768,512]{1,0:T(8,128)(2,1)} %get-tuple-element.19.d0, bf16[768,512]{1,0:T(8,128)(2,1)} %copy-done.2, bf16[768,512]{1,0:T(8,128)(2,1)} %copy-done.3, bf16[768,512]{1,0:T(8,128)(2,1)} %collective-permute-done.6.do, bf16[512,2048]{1,0:T(8,128)(2,1)} %ps.3, ...), custom_call_target="tpu_custom_call" | custom-call | tf_op jit(solution)/shard_map/tokens/pallas_call | solution.py:171
  170.7 2.8 %collective-permute-start.3 = (f32[16]{0:T(128)S(1)}, f32[16]{0:T(128)S(1)}, u32[]{:S(2)}, u32[]{:S(2)}) collective-permute-start(f32[16]{0:T(128)S(1)} %multiply_reduce_fusion), channel_id=1, source_target_pairs={{0,1},{1,0},{2,3},{3,2},{4,5},{5,4},{6,7},{7,6},{8,9},{9,8},{10,11... | collective-permute-start | bytes 200 | tf_op jit(solution)/shard_map/ppermute | solution.py:19
  (67 shorter events, 21.6 us)
Async XLA Ops:
  12.8 5.4 %collective-permute-start = (f32[1,2560]{1,0:T(1,128)}, f32[1,2560]{1,0:T(1,128)S(1)}, u32[]{:S(2)}, u32[]{:S(2)}) collective-permute-start(f32[1,2560]{1,0:T(1,128)} %get-tuple-element.14.mine.refs_13_), channel_id=1, source_target_pairs={{0,1},{1,0},{2,3},{3,2},{4,5},{5,4},{6,7},{7,6},{8,9},{9,8},{10,11... | collective-permute-start | bytes 30728 | tf_op jit(solution)/shard_map/ppermute | solution.py:19
  22.0 19.8 %collective-permute-start.1 = (bf16[768,512]{1,0:T(8,128)(2,1)}, bf16[768,512]{1,0:T(8,128)(2,1)S(1)}, u32[]{:S(2)}, u32[]{:S(2)}) collective-permute-start(bf16[768,512]{1,0:T(8,128)(2,1)} %part.1), channel_id=1, source_target_pairs={{0,1},{1,0},{2,3},{3,2},{4,5},{5,4},{6,7},{7,6},{8,9},{9,8},{10,11... | collective-permute-start | bytes 2359304 | tf_op jit(solution)/shard_map/ppermute | solution.py:19
  52.9 3.2 %collective-permute-start.2 = (bf16[16,16,2176]{2,1,0:T(8,128)(2,1)}, bf16[16,16,2176]{2,1,0:T(8,128)(2,1)S(1)}, u32[]{:S(2)}, u32[]{:S(2)}) collective-permute-start(bf16[16,16,2176]{2,1,0:T(8,128)(2,1)} %get-tuple-element.18), channel_id=1, source_target_pairs={{0,2},{2,0},{4,6},{6,4},{8,10},{10,8},{12,14},{14,12},{16,18},{18,... | collective-permute-start | bytes 3342344 | tf_op jit(solution)/shard_map/ppermute | solution.py:27
  54.0 18.5 %collective-permute-start.7 = (bf16[128,2048]{1,0:T(8,128)(2,1)S(1)}, bf16[128,2048]{1,0:T(8,128)(2,1)S(1)}, u32[]{:S(2)}, u32[]{:S(2)}) collective-permute-start(bf16[128,2048]{1,0:T(8,128)(2,1)S(1)} %constant_dynamic-slice_fusion), channel_id=1, source_target_pairs={{0,64},{64,128},{128,192},{192,0},{1,65},{65,129},{129,193},{193,1... | collective-permute-start | bytes 1572872 | tf_op jit(solution)/shard_map/ppermute | solution.py:15
  55.7 18.7 %collective-permute-start.8 = (bf16[128,2048]{1,0:T(8,128)(2,1)S(1)}, bf16[128,2048]{1,0:T(8,128)(2,1)}, u32[]{:S(2)}, u32[]{:S(2)}) collective-permute-start(bf16[128,2048]{1,0:T(8,128)(2,1)S(1)} %constant_dynamic-slice_fusion), channel_id=1, source_target_pairs={{0,192},{64,0},{128,64},{192,128},{1,193},{65,1},{129,65},{193,129... | collective-permute-start | bytes 1572872 | tf_op jit(solution)/shard_map/ppermute | solution.py:15
  60.5 59.7 %copy-start.1 = (bf16[768,512]{1,0:T(8,128)(2,1)S(1)}, bf16[768,512]{1,0:T(8,128)(2,1)}, u32[]{:S(2)}) copy-start(bf16[768,512]{1,0:T(8,128)(2,1)} %get-tuple-element.19.d0) | copy-start | bytes 2359300
  60.5 109.0 %all-to-all-start = ((bf16[16,16,2176]{2,1,0:T(8,128)(2,1)}), bf16[16,16,2176]{2,1,0:T(8,128)(2,1)S(1)}, u32[]{:S(2)}, u32[]{:S(2)}) async-start(bf16[16,16,2176]{2,1,0:T(8,128)(2,1)} %join.1), calls=%async_computation | async-start | bytes 2228224 | tf_op jit(solution)/shard_map/all_to_all | solution.py:226
  70.1 16.7 %collective-permute-start.9 = (bf16[128,2048]{1,0:T(8,128)(2,1)S(1)}, bf16[128,2048]{1,0:T(8,128)(2,1)S(1)}, u32[]{:S(2)}, u32[]{:S(2)}) collective-permute-start(bf16[128,2048]{1,0:T(8,128)(2,1)S(1)} %constant_dynamic-slice_fusion), channel_id=1, source_target_pairs={{0,128},{64,192},{128,0},{192,64},{1,129},{65,193},{129,1},{193,65... | collective-permute-start | bytes 1572872 | tf_op jit(solution)/shard_map/ppermute | solution.py:15
  72.5 37.3 %collective-permute-start.10 = (bf16[128,2048]{1,0:T(8,128)(2,1)S(1)}, bf16[128,2048]{1,0:T(8,128)(2,1)S(1)}, u32[]{:S(2)}, u32[]{:S(2)}) collective-permute-start(bf16[128,2048]{1,0:T(8,128)(2,1)S(1)} %collective-permute-done.7.refs_0_), channel_id=1, source_target_pairs={{0,4},{2,6},{4,8},{6,10},{8,12},{10,14},{12,16},{14,18},{16,20},{1... | collective-permute-start | bytes 1572872 | tf_op jit(solution)/shard_map/ppermute | solution.py:27
  74.4 35.5 %collective-permute-start.11 = (bf16[128,2048]{1,0:T(8,128)(2,1)}, bf16[128,2048]{1,0:T(8,128)(2,1)}, u32[]{:S(2)}, u32[]{:S(2)}) collective-permute-start(bf16[128,2048]{1,0:T(8,128)(2,1)} %collective-permute-done.8.refs_1_), channel_id=1, source_target_pairs={{0,28},{2,30},{4,0},{6,2},{8,4},{10,6},{12,8},{14,10},{16,12},{18,... | collective-permute-start | bytes 1572872 | tf_op jit(solution)/shard_map/ppermute | solution.py:27
  75.8 5.3 %collective-permute-start.19 = (f32[1,768]{1,0:T(1,128)S(1)}, f32[1,768]{1,0:T(1,128)S(1)}, u32[]{:S(2)}, u32[]{:S(2)}) collective-permute-start(f32[1,768]{1,0:T(1,128)S(1)} %copy-done.13), channel_id=1, source_target_pairs={{0,1},{1,0},{2,3},{3,2},{4,5},{5,4},{6,7},{7,6},{8,9},{9,8},{10,11... | collective-permute-start | bytes 9224 | tf_op jit(solution)/shard_map/ppermute | solution.py:19
  81.1 4.3 %collective-permute-start.20 = (f32[1,768]{1,0:T(1,128)S(1)}, f32[1,768]{1,0:T(1,128)S(1)}, u32[]{:S(2)}, u32[]{:S(2)}) collective-permute-start(f32[1,768]{1,0:T(1,128)S(1)} %add.66), channel_id=1, source_target_pairs={{0,64},{64,128},{128,192},{192,0},{1,65},{65,129},{129,193},{193,1... | collective-permute-start | bytes 9224 | tf_op jit(solution)/shard_map/ppermute | solution.py:15
  85.4 5.1 %collective-permute-start.21 = (f32[1,768]{1,0:T(1,128)S(1)}, f32[1,768]{1,0:T(1,128)S(1)}, u32[]{:S(2)}, u32[]{:S(2)}) collective-permute-start(f32[1,768]{1,0:T(1,128)S(1)} %add.67), channel_id=1, source_target_pairs={{0,128},{64,192},{128,0},{192,64},{1,129},{65,193},{129,1},{193,65... | collective-permute-start | bytes 9224 | tf_op jit(solution)/shard_map/ppermute | solution.py:15
  86.8 33.4 %collective-permute-start.12 = (bf16[128,2048]{1,0:T(8,128)(2,1)S(1)}, bf16[128,2048]{1,0:T(8,128)(2,1)}, u32[]{:S(2)}, u32[]{:S(2)}) collective-permute-start(bf16[128,2048]{1,0:T(8,128)(2,1)S(1)} %collective-permute-done.9.refs_2_), channel_id=1, source_target_pairs={{0,4},{2,6},{4,8},{6,10},{8,12},{10,14},{12,16},{14,18},{16,20},{1... | collective-permute-start | bytes 1572872 | tf_op jit(solution)/shard_map/ppermute | solution.py:27
  88.1 33.7 %collective-permute-start.13 = (bf16[128,2048]{1,0:T(8,128)(2,1)S(1)}, bf16[128,2048]{1,0:T(8,128)(2,1)S(1)}, u32[]{:S(2)}, u32[]{:S(2)}) collective-permute-start(bf16[128,2048]{1,0:T(8,128)(2,1)S(1)} %collective-permute-done.7.refs_0_), channel_id=1, source_target_pairs={{0,2},{2,0},{4,6},{6,4},{8,10},{10,8},{12,14},{14,12},{16,18},{18,... | collective-permute-start | bytes 1572872 | tf_op jit(solution)/shard_map/ppermute | solution.py:27
  90.5 31.8 %collective-permute-start.14 = (bf16[128,2048]{1,0:T(8,128)(2,1)}, bf16[128,2048]{1,0:T(8,128)(2,1)S(1)}, u32[]{:S(2)}, u32[]{:S(2)}) collective-permute-start(bf16[128,2048]{1,0:T(8,128)(2,1)} %collective-permute-done.8.refs_1_), channel_id=1, source_target_pairs={{0,2},{2,0},{4,6},{6,4},{8,10},{10,8},{12,14},{14,12},{16,18},{18,... | collective-permute-start | bytes 1572872 | tf_op jit(solution)/shard_map/ppermute | solution.py:27
  109.8 14.8 %collective-permute-start.15 = (bf16[128,2048]{1,0:T(8,128)(2,1)S(1)}, bf16[128,2048]{1,0:T(8,128)(2,1)S(1)}, u32[]{:S(2)}, u32[]{:S(2)}) collective-permute-start(bf16[128,2048]{1,0:T(8,128)(2,1)S(1)} %collective-permute-done.9.refs_2_), channel_id=1, source_target_pairs={{0,2},{2,0},{4,6},{6,4},{8,10},{10,8},{12,14},{14,12},{16,18},{18,... | collective-permute-start | bytes 1572872 | tf_op jit(solution)/shard_map/ppermute | solution.py:27
  109.8 14.9 %collective-permute-start.16 = (bf16[128,2048]{1,0:T(8,128)(2,1)S(1)}, bf16[128,2048]{1,0:T(8,128)(2,1)S(1)}, u32[]{:S(2)}, u32[]{:S(2)}) collective-permute-start(bf16[128,2048]{1,0:T(8,128)(2,1)S(1)} %collective-permute-done.10.refs_3_), channel_id=1, source_target_pairs={{0,2},{2,0},{4,6},{6,4},{8,10},{10,8},{12,14},{14,12},{16,18},{18,... | collective-permute-start | bytes 1572872 | tf_op jit(solution)/shard_map/ppermute | solution.py:27
  120.2 20.4 %collective-permute-start.4 = (bf16[768,512]{1,0:T(8,128)(2,1)S(1)}, bf16[768,512]{1,0:T(8,128)(2,1)S(1)}, u32[]{:S(2)}, u32[]{:S(2)}) collective-permute-start(bf16[768,512]{1,0:T(8,128)(2,1)S(1)} %copy-done.1), channel_id=1, source_target_pairs={{0,64},{64,128},{128,192},{192,0},{1,65},{65,129},{129,193},{193,1... | collective-permute-start | bytes 2359304 | tf_op jit(solution)/shard_map/ppermute | solution.py:15
  121.7 19.8 %collective-permute-start.5 = (bf16[768,512]{1,0:T(8,128)(2,1)S(1)}, bf16[768,512]{1,0:T(8,128)(2,1)S(1)}, u32[]{:S(2)}, u32[]{:S(2)}) collective-permute-start(bf16[768,512]{1,0:T(8,128)(2,1)S(1)} %copy-done.1), channel_id=1, source_target_pairs={{0,192},{64,0},{128,64},{192,128},{1,193},{65,1},{129,65},{193,129... | collective-permute-start | bytes 2359304 | tf_op jit(solution)/shard_map/ppermute | solution.py:15
  122.3 35.5 %collective-permute-start.6 = (bf16[768,512]{1,0:T(8,128)(2,1)S(1)}, bf16[768,512]{1,0:T(8,128)(2,1)}, u32[]{:S(2)}, u32[]{:S(2)}) collective-permute-start(bf16[768,512]{1,0:T(8,128)(2,1)S(1)} %copy-done.1), channel_id=1, source_target_pairs={{0,128},{64,192},{128,0},{192,64},{1,129},{65,193},{129,1},{193,65... | collective-permute-start | bytes 2359304 | tf_op jit(solution)/shard_map/ppermute | solution.py:15
  124.6 3.6 %collective-permute-start.17 = (bf16[128,2048]{1,0:T(8,128)(2,1)}, bf16[128,2048]{1,0:T(8,128)(2,1)}, u32[]{:S(2)}, u32[]{:S(2)}) collective-permute-start(bf16[128,2048]{1,0:T(8,128)(2,1)} %collective-permute-done.11.refs_4_), channel_id=1, source_target_pairs={{0,2},{2,0},{4,6},{6,4},{8,10},{10,8},{12,14},{14,12},{16,18},{18,... | collective-permute-start | bytes 1572872 | tf_op jit(solution)/shard_map/ppermute | solution.py:27
  126.2 2.3 %collective-permute-start.18 = (bf16[128,2048]{1,0:T(8,128)(2,1)}, bf16[128,2048]{1,0:T(8,128)(2,1)}, u32[]{:S(2)}, u32[]{:S(2)}) collective-permute-start(bf16[128,2048]{1,0:T(8,128)(2,1)} %collective-permute-done.12.refs_5_), channel_id=1, source_target_pairs={{0,2},{2,0},{4,6},{6,4},{8,10},{10,8},{12,14},{14,12},{16,18},{18,... | collective-permute-start | bytes 1572872 | tf_op jit(solution)/shard_map/ppermute | solution.py:27
  170.7 5.2 %collective-permute-start.3 = (f32[16]{0:T(128)S(1)}, f32[16]{0:T(128)S(1)}, u32[]{:S(2)}, u32[]{:S(2)}) collective-permute-start(f32[16]{0:T(128)S(1)} %multiply_reduce_fusion), channel_id=1, source_target_pairs={{0,1},{1,0},{2,3},{3,2},{4,5},{5,4},{6,7},{7,6},{8,9},{9,8},{10,11... | collective-permute-start | bytes 200 | tf_op jit(solution)/shard_map/ppermute | solution.py:19
  (13 other events, 160.0 us)

commit v2 on v1

v2 whole, which is shorter than its diff:
```python
import jax
import jax.numpy as jnp
from jax import lax
from jax.experimental import pallas as pl
from jax.experimental.pallas import tpu as pltpu
from jax.sharding import PartitionSpec as P


epsilon = 1e-06
bf16, f32 = jnp.bfloat16, jnp.float32
SMEM = pl.BlockSpec(memory_space=pltpu.SMEM)


def row_shift(x, by):
    return lax.ppermute(x, "row", [(i, (i + by) % 4) for i in range(4)])


def feat_swap(x):
    return lax.ppermute(x, "feat", [(0, 1), (1, 0)])


def col_move(x, move):
    def target(c):
        a, z, k = move(c // 16, (c // 2) % 8, c % 2)
        return a * 16 + z * 2 + k

    return lax.ppermute(x, "col", [(c, target(c)) for c in range(32)])


def core_swap(x):
    return col_move(x, lambda a, z, k: (a, z, 1 - k))


def deep_shift(x, by):
    return col_move(x, lambda a, z, k: (a, (z + by) % 8, k))


def fold_lanes(x):
    return sum(x[:, i : i + 128] for i in range(0, x.shape[1], 128))


def to_row(x):
    return jnp.sum(x.T, axis=0, keepdims=True)


def column(row, copies):
    tall = jnp.broadcast_to(row, (128, row.shape[1])).T
    return jnp.concatenate([tall] * copies, axis=1)


def shape(dims, dtype):
    return jax.ShapeDtypeStruct(dims, dtype)


def norm_kernel(ps, pt, ts, tt, sums, squares):
    step = pl.program_id(0)

    @pl.when(step == 0)
    def _():
        squares[...] = jnp.zeros_like(squares)

    start = 0
    for ref in (ps, pt, ts, tt):
        values = ref[...].astype(f32)
        rows = slice(start, start + values.shape[0])
        squares[rows] += fold_lanes(values * values)
        start += values.shape[0]

    @pl.when(step == pl.num_programs(0) - 1)
    def _():
        sums[...] = to_row(squares[...])


def strip(a, width=512, last=None):
    if last is None:
        return pl.BlockSpec((a.shape[0], width), lambda i: (0, i))
    return pl.BlockSpec((a.shape[0], width), lambda i: (0, jnp.minimum(i, last)))


def whole(a):
    return pl.BlockSpec(a.shape, lambda i: (0,) * len(a.shape))


def norms(*features):
    return pl.pallas_call(
        norm_kernel,
        grid=(4,),
        out_shape=shape((1, 2560), f32),
        in_specs=[strip(a) for a in features],
        out_specs=pl.BlockSpec((1, 2560), lambda i: (0, 0)),
        scratch_shapes=[pltpu.VMEM((2560, 128), f32)],
        name="norms",
    )(*features)


def gram_kernel(ps, pt, ts, tt, student, teacher):
    def inner(left, right):
        return lax.dot_general(left[...], right[...], (((1,), (1,)), ((), ())), preferred_element_type=f32)

    student[...] = inner(ts, ps)
    teacher[...] = inner(tt, pt)


def tall(width):
    return pl.BlockSpec((256, width), lambda i: (i, 0))


def grams(ps, pt, ts, tt):
    return pl.pallas_call(
        gram_kernel,
        grid=(3,),
        out_shape=[shape((768, 512), f32)] * 2,
        in_specs=[whole(ps), whole(pt), tall(2048), tall(2048)],
        out_specs=[tall(512)] * 2,
        name="grams",
    )(ps, pt, ts, tt)


SUMS = (
    pl.BlockSpec((1, 512), lambda i: (0, 0)),
    pl.BlockSpec((1, 512), lambda i: (0, 1)),
    pl.BlockSpec((1, 256), lambda i: (0, 4 + i)),
    pl.BlockSpec((1, 256), lambda i: (0, 7 + i)),
)


def inverse(total):
    return 1.0 / jnp.sqrt(total + epsilon)


def scaled(student, teacher, sums):
    inv_ps, inv_pt, inv_ts, inv_tt = (inverse(a[...] + b[...]) for a, b in zip(sums[:4], sums[4:]))
    scale = column(inv_ts, 4)
    near = student[...] * inv_ps * scale
    return near, near - teacher[...] * inv_pt * column(inv_tt, 4), inv_ps, scale


def part_kernel(student, teacher, *refs):
    refs[8][...] = scaled(student, teacher, refs[:8])[1].astype(bf16)


def part_of(student, teacher, mine, other):
    return pl.pallas_call(
        part_kernel,
        grid=(3,),
        out_shape=shape((768, 512), bf16),
        in_specs=[tall(512)] * 2 + [*SUMS, *SUMS],
        out_specs=tall(512),
        name="part",
    )(student, teacher, *([mine] * 4), *([other] * 4))


def mismatch_kernel(student, teacher, *refs):
    partner, doubled, weighted, loss, sides = refs[8:]
    step = pl.program_id(0)
    near, part, inv_ps, scale = scaled(student, teacher, refs[:8])
    mismatch = part + partner[...].astype(f32)
    twice = 2.0 * mismatch
    doubled[...] = (twice * inv_ps).astype(bf16)
    weighted[...] = (twice * scale).astype(bf16).T
    product = twice * near

    @pl.when(step == 0)
    def _():
        loss[...] = jnp.zeros_like(loss)
        sides[...] = jnp.zeros_like(sides)

    loss[...] += jnp.sum(mismatch * mismatch, axis=0, keepdims=True)
    sides[:, :512] += jnp.sum(product, axis=0, keepdims=True)
    sides[:, pl.ds(pl.multiple_of(512 + step * 256, 256), 256)] = to_row(fold_lanes(product))


def mismatch_of(student, teacher, mine, other, partner):
    return pl.pallas_call(
        mismatch_kernel,
        grid=(3,),
        out_shape=[shape((768, 512), bf16), shape((512, 768), bf16), shape((1, 512), f32), shape((1, 1280), f32)],
        in_specs=[tall(512)] * 2 + [*SUMS, *SUMS] + [tall(512)],
        out_specs=[
            tall(512),
            pl.BlockSpec((512, 256), lambda i: (0, i)),
            pl.BlockSpec((1, 512), lambda i: (0, 0)),
            pl.BlockSpec((1, 1280), lambda i: (0, 0)),
        ],
        name="mismatch",
    )(student, teacher, *([mine] * 4), *([other] * 4), partner)


def pick(weighted, core, ts):
    return jnp.dot(weighted[:, core].reshape(256, 768), ts[...], preferred_element_type=f32)


def away_kernel(core, weighted, ts, away):
    away[...] = pick(weighted, 1 - core[0], ts).astype(bf16)


def away_of(core, weighted, ts):
    return pl.pallas_call(
        away_kernel,
        grid=(4,),
        out_shape=shape((256, 2048), bf16),
        in_specs=[SMEM, whole(weighted), strip(ts)],
        out_specs=pl.BlockSpec((256, 512), lambda i: (0, i)),
        name="away",
    )(core, weighted, ts)


def join_kernel(core, weighted, ts, away, mine, other, out):
    step = pl.program_id(0)

    @pl.when(step < 4)
    def _():
        total = pick(weighted, core[0], ts) + away[...].astype(f32)
        out[...] = total.astype(bf16).reshape(16, 16, 512)

    @pl.when(step == 4)
    def _():
        stats = mine[...] + other[...]
        lane = lax.broadcasted_iota(jnp.int32, (512, 128), 1)
        tile = jnp.zeros((512, 128), f32)
        for row in range(2):
            total = column(stats[row : row + 1], 1)
            high = total.astype(bf16).astype(f32)
            tile = jnp.where(lane == 2 * row, high, jnp.where(lane == 2 * row + 1, total - high, tile))
        tile = tile.reshape(16, 2, 16, 128)
        out[:, :, :128] = jnp.where(core[0] == 0, tile[:, 0], tile[:, 1]).astype(bf16)


def join_of(core, weighted, ts, away, mine, other):
    return pl.pallas_call(
        join_kernel,
        grid=(5,),
        out_shape=shape((16, 16, 2176), bf16),
        in_specs=[SMEM, whole(weighted), strip(ts, last=3), strip(away, last=3), whole(mine), whole(other)],
        out_specs=pl.BlockSpec((16, 16, 512), lambda i: (0, 0, i)),
        name="join",
    )(core, weighted, ts, away, mine, other)


def final_kernel(spread, ps, inverses, loss, out):
    total = spread[0].astype(f32)
    for i in range(1, 16):
        total += spread[i].astype(f32)
    term, stats = total[:, :2048], total[:, 2048:]
    along = stats[:, 2:3] + stats[:, 3:4]
    unit = ps[...].astype(f32) * inverses[...]
    out[...] = ((term - unit * along) * inverses[...]).astype(bf16)
    turned = jnp.concatenate([stats, jnp.zeros((112, 128), f32)], axis=0).T
    loss[...] = (turned[0:1] + turned[1:2])[:, :16]


def final(spread, ps, inverses):
    return pl.pallas_call(
        final_kernel,
        out_shape=[shape((1, 16), f32), shape((16, 2048), bf16)],
        name="final",
    )(spread, ps, inverses)


def token_kernel(place, d0, dl, dr, do, ps, *refs):
    pieces, (ts, mine, other, a0, a1, a2, a3, out, work, twice) = refs[:12], refs[12:]
    deep, core = place[0], place[1]

    @pl.when(pl.program_id(0) == 0)
    def _():
        for i, ref in enumerate((d0, dl, dr, do)):
            twice[:, i * 512 : i * 512 + 512] = ref[...]

    work[:512] = ps[...]
    for order, (a, b) in enumerate(((deep, core), (1 - deep, core), (deep, 1 - core), (1 - deep, 1 - core))):
        for side in range(3):
            start = pl.multiple_of(512 * side + 512 + (a * 2 + b) * 128, 128)
            work[pl.ds(start, 128)] = pieces[order * 3 + side][...]
    total = jnp.dot(twice[...], work[...], preferred_element_type=f32)
    inv_ts = inverse(mine[...] + other[...])[:, 1024:1792]
    along = a0[...] + a1[...] + a2[...] + a3[...]
    copies = ts.shape[1] // 128
    out[...] = (total * column(inv_ts, copies) - ts[...].astype(f32) * column(inv_ts * inv_ts * along, copies)).astype(bf16)


def token_grad(place, doubled, ps, pieces, ts, mine, other, along):
    return pl.pallas_call(
        token_kernel,
        grid=(4,),
        out_shape=shape(ts.shape, bf16),
        in_specs=[SMEM]
        + [whole(a) for a in doubled]
        + [strip(a) for a in (ps, *pieces, ts)]
        + [whole(a) for a in (mine, other, *along)],
        out_specs=strip(ts),
        scratch_shapes=[pltpu.VMEM((2048, 512), bf16), pltpu.VMEM((768, 2048), bf16)],
        name="tokens",
    )(place, *doubled, ps, *pieces, ts, mine, other, *along)


def local(panel_student, panel_teacher, tokens_student, tokens_teacher):
    col = lax.axis_index("col")
    deep, core = (col // 2) % 2, col % 2
    place = jnp.stack([deep, core]).astype(jnp.int32)
    index = core.astype(jnp.int32)[None]
    features = (panel_student, panel_teacher, tokens_student, tokens_teacher)

    mine = norms(*features)
    other = feat_swap(mine)
    student, teacher = grams(*features)
    part = part_of(student, teacher, mine, other)
    held, part = lax.optimization_barrier((panel_student, part))
    partner = feat_swap(part)

    quarter = lax.dynamic_slice_in_dim(held, (deep * 2 + core) * 128, 128, 0)
    left = row_shift(quarter, 1)
    right = row_shift(quarter, 3)
    far = row_shift(quarter, 2)
    first = (left, right, far)
    second = (deep_shift(left, 1), deep_shift(right, 7), deep_shift(far, 1))
    third = tuple(core_swap(a) for a in first)
    fourth = tuple(core_swap(a) for a in second)
    pieces = first + second + third + fourth

    doubled, weighted, loss, sides = mismatch_of(student, teacher, mine, other, partner)
    gathered = (doubled, row_shift(doubled, 1), row_shift(doubled, 3), row_shift(doubled, 2))
    weighted = weighted.reshape(16, 2, 16, 768)
    away = away_of(index, weighted, tokens_student)
    away = core_swap(away)

    sides += feat_swap(sides)
    stats = jnp.concatenate([loss, sides[:, :512]], axis=0)
    stats_other = core_swap(stats)
    along = sides[:, 512:]
    along = (along,) + tuple(row_shift(along, i) for i in (1, 2, 3))

    joined = join_of(index, weighted, tokens_student, away, stats, stats_other)
    groups = [[a * 16 + z * 2 + k for a in range(2) for z in range(8)] for k in range(2)]
    spread = lax.all_to_all(joined, "col", 0, 0, axis_index_groups=groups, tiled=True)

    grad_tokens = token_grad(place, gathered, panel_student, pieces, tokens_student, mine, other, along)

    rows = lambda a: lax.dynamic_slice_in_dim(a, col * 16, 16, 0)
    inv_rows = inverse(rows(mine[0]) + rows(other[0]))[:, None]
    row_loss, grad_panel = final(spread, rows(panel_student), inv_rows)
    return (row_loss.reshape(16), grad_panel, grad_tokens)


def solution(mesh):
    placed = (P("row", "feat"), P("row", "feat"), P("col", "feat"), P("col", "feat"))
    return jax.shard_map(
        local,
        mesh=mesh,
        in_specs=placed,
        out_specs=(P(("row", "col")), P(("row", "col"), "feat"), P("col", "feat")),
        check_vma=False,
    )
```

time: 179 us -> 180 us (level)
  Pallas kernels: 40.7 us -> 47.1 us
  starting transfers between devices: 37.9 us -> 31.8 us
  other arithmetic: 5.48 us -> 1.3 us
  local copies, waits for them, and re-layouts: 5.06 us -> 8.84 us
    ppermute x4 -> x3, starting transfers between devices: 11.8 us -> 4.12 us  [feat_swap(): return lax.ppermute(x, 'feat', [(0, 1), (1, 0)])]
    pallas_call x6 -> x8, Pallas kernels: 40.7 us -> 47.1 us  [the longest x1 12.1 us: token_grad(): pl.pallas_call(token_kernel, grid=(4,), out_shape=shape(ts.shape, bf16),...]
    ppermute x10 -> x11, waiting for transfers between devices: 29.4 us -> 32 us  [col_move(): return lax.ppermute(x, 'col', [(c, target(c)) for c in range(32)])]
    ppermute x8 -> x9, starting transfers between devices: 11.3 us -> 13.5 us  [row_shift(): return lax.ppermute(x, 'row', [(i, (i + by) % 4) for i in range(4)])]
    unnamed x28 -> x44, local copies, waits for them, and re-layouts: 3.98 us -> 5.61 us
    ppermute x4 -> x3, waiting for transfers between devices: 23.2 us -> 21.6 us  [feat_swap(): return lax.ppermute(x, 'feat', [(0, 1), (1, 0)])]
    ppermute x10 -> x11, starting transfers between devices: 5.1 us -> 5.5 us  [col_move(): return lax.ppermute(x, 'col', [(c, target(c)) for c in range(32)])]
    ppermute x8 -> x9, waiting for transfers between devices: 35.1 us -> 35.2 us  [row_shift(): return lax.ppermute(x, 'row', [(i, (i + by) % 4) for i in range(4)])]
  transfers between devices with their start and end apart: 23 -> 24, of which waited for: 12 -> 10; matrix products, arithmetic and copies ran while one was open for 2% -> 3% of each run, Pallas kernels for 9% -> 14%
where the time goes in v2:
time: 180 us; the launch traced here: 179 us
  waiting for transfers between devices  88.8 us (49%)
  Pallas kernels  47.1 us (26%)
  starting transfers between devices  31.8 us (18%)
  local copies, waits for them, and re-layouts  8.84 us (5%)
    ppermute x9, waiting for transfers between devices, row_shift(): return lax.ppermute(x, 'row', [(i, (i + by) % 4) for i in range(4)])  35.2 us
    ppermute x11, waiting for transfers between devices, col_move(): return lax.ppermute(x, 'col', [(c, target(c)) for c in range(32)])  32 us
    ppermute x3, waiting for transfers between devices, feat_swap(): return lax.ppermute(x, 'feat', [(0, 1), (1, 0)])  21.6 us
    ppermute x9, starting transfers between devices, row_shift(): return lax.ppermute(x, 'row', [(i, (i + by) % 4) for i in range(4)])  13.5 us
    pallas_call x1, Pallas kernels, token_grad(): pl.pallas_call(token_kernel, grid=(4,), out_shape=shape(ts.shape, bf16),...  12.1 us
    all_to_all x1, starting transfers between devices, local(): lax.all_to_all(joined, 'col', 0, 0, axis_index_groups=groups, tiled=True)  8.73 us
    pallas_call x1, Pallas kernels, grams(): pl.pallas_call(gram_kernel, grid=(3,), out_shape=[shape((768, 512), f32)]...  8.11 us
    pallas_call x1, Pallas kernels, norms(): pl.pallas_call(norm_kernel, grid=(4,), out_shape=shape((1, 2560), f32), i...  6.52 us
  transfers between devices with their start and end apart: 24, of which 10 were waited for; matrix products, arithmetic and copies ran while one was open for 3% of the time, Pallas kernels for 14%

profile of v2, /device:TPU:8, one launch (start us, length us, event | category | flops | bytes accessed | tf_op | source)
XLA Modules:
  0.0 178.8 jit_solution(11662244108303544075)
XLA Ops:
  0.6 6.5 %norms.1.refs_0_.refs_1_.refs_2_.refs_3_.refs_13_ = f32[1,2560]{1,0:T(1,128)} custom-call(bf16[512,2048]{1,0:T(8,128)(2,1)} %ps.5, bf16[512,2048]{1,0:T(8,128)(2,1)} %pt.3, bf16[768,2048]{1,0:T(8,128)(2,1)} %refs_12_.1, bf16[768,2048]{1,0:T(8,128)(2,1)} %tt.3), custom_call_target="tpu_custom_call" | custom-call | tf_op jit(solution)/shard_map/norms/pallas_call | solution.py:85
  7.1 3.0 %collective-permute-start = (f32[1,2560]{1,0:T(1,128)}, f32[1,2560]{1,0:T(1,128)S(1)}, u32[]{:S(2)}, u32[]{:S(2)}) collective-permute-start(f32[1,2560]{1,0:T(1,128)} %norms.1.refs_0_.refs_1_.refs_2_.refs_3_.refs_13_), channel_id=1, source_target_pairs={{0,1},{1,0},{2,3},{3,2},{4,5},{5,4},{6,7},{7,6},{8,9},{9,8},{10,11... | collective-permute-start | bytes 30728 | tf_op jit(solution)/shard_map/ppermute | solution.py:19
  10.2 8.1 %grams.1 = (f32[768,512]{1,0:T(8,128)}, f32[768,512]{1,0:T(8,128)}) custom-call(bf16[512,2048]{1,0:T(8,128)(2,1)} %ps.5, bf16[512,2048]{1,0:T(8,128)(2,1)} %pt.3, bf16[768,2048]{1,0:T(8,128)(2,1)} %refs_12_.1, bf16[768,2048]{1,0:T(8,128)(2,1)} %tt.3), custom_call_target="tpu_custom_call" | custom-call | tf_op jit(solution)/shard_map/grams/pallas_call | solution.py:109
  18.9 3.8 %part.1 = bf16[768,512]{1,0:T(8,128)(2,1)} custom-call(f32[768,512]{1,0:T(8,128)} %get-tuple-element.13.student, f32[768,512]{1,0:T(8,128)} %get-tuple-element.14.teacher, f32[1,2560]{1,0:T(1,128)} %norms.1.refs_0_.refs_1_.refs_2_.refs_3_.refs_13_, f32[1,2560]{1,0:T(1,128)} %norms.1.refs_0_.refs_1_.refs_2_.refs_3_.refs_13_, ...), custom_call_target="tpu_custom_call" | custom-call | tf_op jit(solution)/shard_map/part/pallas_call | solution.py:143
  23.2 20.2 %collective-permute-done.1.refs_8_ = bf16[768,512]{1,0:T(8,128)(2,1)S(1)} collective-permute-done((bf16[768,512]{1,0:T(8,128)(2,1)}, bf16[768,512]{1,0:T(8,128)(2,1)S(1)}, u32[]{:S(2)}, u32[]{:S(2)}) %collective-permute-start.1) | collective-permute-done | bytes 786464 | tf_op jit(solution)/shard_map/ppermute | solution.py:19
  44.3 4.5 %mismatch.1 = (bf16[768,512]{1,0:T(8,128)(2,1)}, bf16[512,768]{1,0:T(8,128)(2,1)}, f32[1,512]{1,0:T(1,128)}, f32[1,1280]{1,0:T(1,128)}) custom-call(f32[768,512]{1,0:T(8,128)} %get-tuple-element.13.student, f32[768,512]{1,0:T(8,128)} %get-tuple-element.14.teacher, f32[1,2560]{1,0:T(1,128)} %norms.1.refs_0_.refs_1_.refs_2_.refs_3_.refs_13_, ...), custom_call_target="tpu_custom_call" | custom-call | tf_op jit(solution)/shard_map/mismatch/pallas_call | solution.py:174
  48.8 4.7 %away.1 = bf16[256,2048]{1,0:T(8,128)(2,1)} custom-call(s32[1]{0:T(128)} %bitcast.core, bf16[16,2,16,768]{3,2,1,0:T(8,128)(2,1)} %bitcast.6, bf16[768,2048]{1,0:T(8,128)(2,1)} %refs_12_.1), custom_call_target="tpu_custom_call" | custom-call | tf_op jit(solution)/shard_map/away/pallas_call | solution.py:198
  55.2 1.7 collective-permute-start.8
  61.6 5.2 %join.1 = bf16[16,16,2176]{2,1,0:T(8,128)(2,1)} custom-call(s32[1]{0:T(128)} %bitcast.core, bf16[16,2,16,768]{3,2,1,0:T(8,128)(2,1)} %bitcast.7, bf16[768,2048]{1,0:T(8,128)(2,1)} %refs_12_.1, bf16[256,2048]{1,0:T(8,128)(2,1)} %copy-done.1, f32[2,512]{1,0:T(2,128)} %copy-done.14, f32[2,512]{1,0:T(2,128)} %copy-done.17), custom_call_target="tpu_custom_call" | custom-call | tf_op jit(solution)/shard_map/join/pallas_call | solution.py:230
  66.8 8.7 %all-to-all-start = ((bf16[16,16,2176]{2,1,0:T(8,128)(2,1)}), bf16[16,16,2176]{2,1,0:T(8,128)(2,1)S(1)}, u32[]{:S(2)}, u32[]{:S(2)}) async-start(bf16[16,16,2176]{2,1,0:T(8,128)(2,1)} %join.1), calls=%async_computation | async-start | bytes 2228224 | tf_op jit(solution)/shard_map/all_to_all | solution.py:334
  75.6 2.4 %collective-permute-start.10 = (bf16[128,2048]{1,0:T(8,128)(2,1)S(1)}, bf16[128,2048]{1,0:T(8,128)(2,1)S(1)}, u32[]{:S(2)}, u32[]{:S(2)}) collective-permute-start(bf16[128,2048]{1,0:T(8,128)(2,1)S(1)} %constant_dynamic-slice_fusion), channel_id=1, source_target_pairs={{0,128},{64,192},{128,0},{192,64},{1,129},{65,193},{129,1},{193,65... | collective-permute-start | bytes 1572872 | tf_op jit(solution)/shard_map/ppermute | solution.py:15
  78.0 1.8 %collective-permute-start.11 = (bf16[128,2048]{1,0:T(8,128)(2,1)S(1)}, bf16[128,2048]{1,0:T(8,128)(2,1)S(1)}, u32[]{:S(2)}, u32[]{:S(2)}) collective-permute-start(bf16[128,2048]{1,0:T(8,128)(2,1)S(1)} %collective-permute-done.8.refs_0_), channel_id=1, source_target_pairs={{0,4},{2,6},{4,8},{6,10},{8,12},{10,14},{12,16},{14,18},{16,20},{1... | collective-permute-start | bytes 1572872 | tf_op jit(solution)/shard_map/ppermute | solution.py:27
  81.5 3.1 %collective-permute-start.21 = (f32[1,768]{1,0:T(1,128)S(1)}, f32[1,768]{1,0:T(1,128)S(1)}, u32[]{:S(2)}, u32[]{:S(2)}) collective-permute-start(f32[1,768]{1,0:T(1,128)S(1)} %slice.9.refs_15_), channel_id=1, source_target_pairs={{0,128},{64,192},{128,0},{192,64},{1,129},{65,193},{129,1},{193,65... | collective-permute-start | bytes 9224 | tf_op jit(solution)/shard_map/ppermute | solution.py:15
  84.6 6.3 %collective-permute-done.10.refs_2_ = bf16[128,2048]{1,0:T(8,128)(2,1)S(1)} collective-permute-done((bf16[128,2048]{1,0:T(8,128)(2,1)S(1)}, bf16[128,2048]{1,0:T(8,128)(2,1)S(1)}, u32[]{:S(2)}, u32[]{:S(2)}) %collective-permute-start.10) | collective-permute-done | bytes 524320 | tf_op jit(solution)/shard_map/ppermute | solution.py:15
  92.1 1.6 collective-permute-start.13
  94.5 21.0 %collective-permute-done.11.refs_3_ = bf16[128,2048]{1,0:T(8,128)(2,1)S(1)} collective-permute-done((bf16[128,2048]{1,0:T(8,128)(2,1)S(1)}, bf16[128,2048]{1,0:T(8,128)(2,1)S(1)}, u32[]{:S(2)}, u32[]{:S(2)}) %collective-permute-start.11) | collective-permute-done | bytes 524320 | tf_op jit(solution)/shard_map/ppermute | solution.py:27
  116.0 9.8 %collective-permute-done.13.refs_5_ = bf16[128,2048]{1,0:T(8,128)(2,1)} collective-permute-done((bf16[128,2048]{1,0:T(8,128)(2,1)S(1)}, bf16[128,2048]{1,0:T(8,128)(2,1)}, u32[]{:S(2)}, u32[]{:S(2)}) %collective-permute-start.13) | collective-permute-done | bytes 524320 | tf_op jit(solution)/shard_map/ppermute | solution.py:27
  125.8 1.6 collective-permute-start.5
  127.9 2.3 %collective-permute-start.7 = (bf16[768,512]{1,0:T(8,128)(2,1)S(1)}, bf16[768,512]{1,0:T(8,128)(2,1)}, u32[]{:S(2)}, u32[]{:S(2)}) collective-permute-start(bf16[768,512]{1,0:T(8,128)(2,1)S(1)} %copy-done.3), channel_id=1, source_target_pairs={{0,128},{64,192},{128,0},{192,64},{1,129},{65,193},{129,1},{193,65... | collective-permute-start | bytes 2359304 | tf_op jit(solution)/shard_map/ppermute | solution.py:15
  132.4 1.5 constant_dynamic-slice_fusion.3.ps
  135.3 10.9 %collective-permute-done.5.dl = bf16[768,512]{1,0:T(8,128)(2,1)S(1)} collective-permute-done((bf16[768,512]{1,0:T(8,128)(2,1)S(1)}, bf16[768,512]{1,0:T(8,128)(2,1)S(1)}, u32[]{:S(2)}, u32[]{:S(2)}) %collective-permute-start.5) | collective-permute-done | bytes 786464 | tf_op jit(solution)/shard_map/ppermute | solution.py:15
  147.2 16.3 %collective-permute-done.7.do = bf16[768,512]{1,0:T(8,128)(2,1)} collective-permute-done((bf16[768,512]{1,0:T(8,128)(2,1)S(1)}, bf16[768,512]{1,0:T(8,128)(2,1)}, u32[]{:S(2)}, u32[]{:S(2)}) %collective-permute-start.7) | collective-permute-done | bytes 786464 | tf_op jit(solution)/shard_map/ppermute | solution.py:15
  163.5 12.1 %tokens.1 = bf16[768,2048]{1,0:T(8,128)(2,1)} custom-call(s32[2]{0:T(128)} %pad_add_fusion.place, bf16[768,512]{1,0:T(8,128)(2,1)} %get-tuple-element.21.d0, bf16[768,512]{1,0:T(8,128)(2,1)} %copy-done.4, bf16[768,512]{1,0:T(8,128)(2,1)} %copy-done.5, bf16[768,512]{1,0:T(8,128)(2,1)} %collective-permute-done.7.do, bf16[512,2048]{1,0:T(8,128)(2,1)} %ps.5, ...), custom_call_target="tpu_custom_call" | custom-call | tf_op jit(solution)/shard_map/tokens/pallas_call | solution.py:282
  176.6 2.2 %final.1 = (f32[1,16]{1,0:T(1,128)}, bf16[16,2048]{1,0:T(8,128)(2,1)}) custom-call(bf16[16,16,2176]{2,1,0:T(8,128)(2,1)} %copy-done, bf16[16,2048]{1,0:T(8,128)(2,1)} %constant_dynamic-slice_fusion.3.ps, f32[16,1]{1,0:T(8,128)} %copy.7.inverses), custom_call_target="tpu_custom_call" | custom-call | tf_op jit(solution)/shard_map/final/pallas_call | solution.py:253
  (85 shorter events, 18.7 us)
Async XLA Ops:
  7.1 11.1 %collective-permute-start = (f32[1,2560]{1,0:T(1,128)}, f32[1,2560]{1,0:T(1,128)S(1)}, u32[]{:S(2)}, u32[]{:S(2)}) collective-permute-start(f32[1,2560]{1,0:T(1,128)} %norms.1.refs_0_.refs_1_.refs_2_.refs_3_.refs_13_), channel_id=1, source_target_pairs={{0,1},{1,0},{2,3},{3,2},{4,5},{5,4},{6,7},{7,6},{8,9},{9,8},{10,11... | collective-permute-start | bytes 30728 | tf_op jit(solution)/shard_map/ppermute | solution.py:19
  22.7 20.7 %collective-permute-start.1 = (bf16[768,512]{1,0:T(8,128)(2,1)}, bf16[768,512]{1,0:T(8,128)(2,1)S(1)}, u32[]{:S(2)}, u32[]{:S(2)}) collective-permute-start(bf16[768,512]{1,0:T(8,128)(2,1)} %part.1), channel_id=1, source_target_pairs={{0,1},{1,0},{2,3},{3,2},{4,5},{5,4},{6,7},{7,6},{8,9},{9,8},{10,11... | collective-permute-start | bytes 2359304 | tf_op jit(solution)/shard_map/ppermute | solution.py:19
  53.6 6.5 %collective-permute-start.2 = (bf16[256,2048]{1,0:T(8,128)(2,1)}, bf16[256,2048]{1,0:T(8,128)(2,1)S(1)}, u32[]{:S(2)}, u32[]{:S(2)}) collective-permute-start(bf16[256,2048]{1,0:T(8,128)(2,1)} %away.1), channel_id=1, source_target_pairs={{0,2},{2,0},{4,6},{6,4},{8,10},{10,8},{12,14},{14,12},{16,18},{18,... | collective-permute-start | bytes 3145736 | tf_op jit(solution)/shard_map/ppermute | solution.py:27
  53.6 5.2 %collective-permute-start.3 = (f32[1,1280]{1,0:T(1,128)S(1)}, f32[1,1280]{1,0:T(1,128)S(1)}, u32[]{:S(2)}, u32[]{:S(2)}) collective-permute-start(f32[1,1280]{1,0:T(1,128)S(1)} %copy-done.16), channel_id=1, source_target_pairs={{0,1},{1,0},{2,3},{3,2},{4,5},{5,4},{6,7},{7,6},{8,9},{9,8},{10,11... | collective-permute-start | bytes 15368 | tf_op jit(solution)/shard_map/ppermute | solution.py:19
  55.2 22.7 %collective-permute-start.8 = (bf16[128,2048]{1,0:T(8,128)(2,1)S(1)}, bf16[128,2048]{1,0:T(8,128)(2,1)S(1)}, u32[]{:S(2)}, u32[]{:S(2)}) collective-permute-start(bf16[128,2048]{1,0:T(8,128)(2,1)S(1)} %constant_dynamic-slice_fusion), channel_id=1, source_target_pairs={{0,64},{64,128},{128,192},{192,0},{1,65},{65,129},{129,193},{193,1... | collective-permute-start | bytes 1572872 | tf_op jit(solution)/shard_map/ppermute | solution.py:15
  56.9 22.9 %collective-permute-start.9 = (bf16[128,2048]{1,0:T(8,128)(2,1)S(1)}, bf16[128,2048]{1,0:T(8,128)(2,1)}, u32[]{:S(2)}, u32[]{:S(2)}) collective-permute-start(bf16[128,2048]{1,0:T(8,128)(2,1)S(1)} %constant_dynamic-slice_fusion), channel_id=1, source_target_pairs={{0,192},{64,0},{128,64},{192,128},{1,193},{65,1},{129,65},{193,129... | collective-permute-start | bytes 1572872 | tf_op jit(solution)/shard_map/ppermute | solution.py:15
  58.8 1.3 collective-permute-start.4
  66.8 108.8 %all-to-all-start = ((bf16[16,16,2176]{2,1,0:T(8,128)(2,1)}), bf16[16,16,2176]{2,1,0:T(8,128)(2,1)S(1)}, u32[]{:S(2)}, u32[]{:S(2)}) async-start(bf16[16,16,2176]{2,1,0:T(8,128)(2,1)} %join.1), calls=%async_computation | async-start | bytes 2228224 | tf_op jit(solution)/shard_map/all_to_all | solution.py:334
  75.6 15.3 %collective-permute-start.10 = (bf16[128,2048]{1,0:T(8,128)(2,1)S(1)}, bf16[128,2048]{1,0:T(8,128)(2,1)S(1)}, u32[]{:S(2)}, u32[]{:S(2)}) collective-permute-start(bf16[128,2048]{1,0:T(8,128)(2,1)S(1)} %constant_dynamic-slice_fusion), channel_id=1, source_target_pairs={{0,128},{64,192},{128,0},{192,64},{1,129},{65,193},{129,1},{193,65... | collective-permute-start | bytes 1572872 | tf_op jit(solution)/shard_map/ppermute | solution.py:15
  78.0 37.5 %collective-permute-start.11 = (bf16[128,2048]{1,0:T(8,128)(2,1)S(1)}, bf16[128,2048]{1,0:T(8,128)(2,1)S(1)}, u32[]{:S(2)}, u32[]{:S(2)}) collective-permute-start(bf16[128,2048]{1,0:T(8,128)(2,1)S(1)} %collective-permute-done.8.refs_0_), channel_id=1, source_target_pairs={{0,4},{2,6},{4,8},{6,10},{8,12},{10,14},{12,16},{14,18},{16,20},{1... | collective-permute-start | bytes 1572872 | tf_op jit(solution)/shard_map/ppermute | solution.py:27
  79.8 35.7 %collective-permute-start.12 = (bf16[128,2048]{1,0:T(8,128)(2,1)}, bf16[128,2048]{1,0:T(8,128)(2,1)}, u32[]{:S(2)}, u32[]{:S(2)}) collective-permute-start(bf16[128,2048]{1,0:T(8,128)(2,1)} %collective-permute-done.9.refs_1_), channel_id=1, source_target_pairs={{0,28},{2,30},{4,0},{6,2},{8,4},{10,6},{12,8},{14,10},{16,12},{18,... | collective-permute-start | bytes 1572872 | tf_op jit(solution)/shard_map/ppermute | solution.py:27
  81.2 10.9 %collective-permute-start.20 = (f32[1,768]{1,0:T(1,128)S(1)}, f32[1,768]{1,0:T(1,128)S(1)}, u32[]{:S(2)}, u32[]{:S(2)}) collective-permute-start(f32[1,768]{1,0:T(1,128)S(1)} %slice.9.refs_15_), channel_id=1, source_target_pairs={{0,64},{64,128},{128,192},{192,0},{1,65},{65,129},{129,193},{193,1... | collective-permute-start | bytes 9224 | tf_op jit(solution)/shard_map/ppermute | solution.py:15
  81.5 12.2 %collective-permute-start.21 = (f32[1,768]{1,0:T(1,128)S(1)}, f32[1,768]{1,0:T(1,128)S(1)}, u32[]{:S(2)}, u32[]{:S(2)}) collective-permute-start(f32[1,768]{1,0:T(1,128)S(1)} %slice.9.refs_15_), channel_id=1, source_target_pairs={{0,128},{64,192},{128,0},{192,64},{1,129},{65,193},{129,1},{193,65... | collective-permute-start | bytes 9224 | tf_op jit(solution)/shard_map/ppermute | solution.py:15
  90.9 3.6 %collective-permute-start.22 = (f32[1,768]{1,0:T(1,128)S(1)}, f32[1,768]{1,0:T(1,128)S(1)}, u32[]{:S(2)}, u32[]{:S(2)}) collective-permute-start(f32[1,768]{1,0:T(1,128)S(1)} %slice.9.refs_15_), channel_id=1, source_target_pairs={{0,192},{64,0},{128,64},{192,128},{1,193},{65,1},{129,65},{193,129... | collective-permute-start | bytes 9224 | tf_op jit(solution)/shard_map/ppermute | solution.py:15
  92.1 33.7 %collective-permute-start.13 = (bf16[128,2048]{1,0:T(8,128)(2,1)S(1)}, bf16[128,2048]{1,0:T(8,128)(2,1)}, u32[]{:S(2)}, u32[]{:S(2)}) collective-permute-start(bf16[128,2048]{1,0:T(8,128)(2,1)S(1)} %collective-permute-done.10.refs_2_), channel_id=1, source_target_pairs={{0,4},{2,6},{4,8},{6,10},{8,12},{10,14},{12,16},{14,18},{16,20},{1... | collective-permute-start | bytes 1572872 | tf_op jit(solution)/shard_map/ppermute | solution.py:27
  93.7 33.7 %collective-permute-start.14 = (bf16[128,2048]{1,0:T(8,128)(2,1)S(1)}, bf16[128,2048]{1,0:T(8,128)(2,1)S(1)}, u32[]{:S(2)}, u32[]{:S(2)}) collective-permute-start(bf16[128,2048]{1,0:T(8,128)(2,1)S(1)} %collective-permute-done.8.refs_0_), channel_id=1, source_target_pairs={{0,2},{2,0},{4,6},{6,4},{8,10},{10,8},{12,14},{14,12},{16,18},{18,... | collective-permute-start | bytes 1572872 | tf_op jit(solution)/shard_map/ppermute | solution.py:27
  94.5 33.4 %collective-permute-start.15 = (bf16[128,2048]{1,0:T(8,128)(2,1)}, bf16[128,2048]{1,0:T(8,128)(2,1)S(1)}, u32[]{:S(2)}, u32[]{:S(2)}) collective-permute-start(bf16[128,2048]{1,0:T(8,128)(2,1)} %collective-permute-done.9.refs_1_), channel_id=1, source_target_pairs={{0,2},{2,0},{4,6},{6,4},{8,10},{10,8},{12,14},{14,12},{16,18},{18,... | collective-permute-start | bytes 1572872 | tf_op jit(solution)/shard_map/ppermute | solution.py:27
  115.5 14.8 %collective-permute-start.16 = (bf16[128,2048]{1,0:T(8,128)(2,1)S(1)}, bf16[128,2048]{1,0:T(8,128)(2,1)S(1)}, u32[]{:S(2)}, u32[]{:S(2)}) collective-permute-start(bf16[128,2048]{1,0:T(8,128)(2,1)S(1)} %collective-permute-done.10.refs_2_), channel_id=1, source_target_pairs={{0,2},{2,0},{4,6},{6,4},{8,10},{10,8},{12,14},{14,12},{16,18},{18,... | collective-permute-start | bytes 1572872 | tf_op jit(solution)/shard_map/ppermute | solution.py:27
  115.5 14.9 %collective-permute-start.17 = (bf16[128,2048]{1,0:T(8,128)(2,1)S(1)}, bf16[128,2048]{1,0:T(8,128)(2,1)S(1)}, u32[]{:S(2)}, u32[]{:S(2)}) collective-permute-start(bf16[128,2048]{1,0:T(8,128)(2,1)S(1)} %collective-permute-done.11.refs_3_), channel_id=1, source_target_pairs={{0,2},{2,0},{4,6},{6,4},{8,10},{10,8},{12,14},{14,12},{16,18},{18,... | collective-permute-start | bytes 1572872 | tf_op jit(solution)/shard_map/ppermute | solution.py:27
  125.8 20.4 %collective-permute-start.5 = (bf16[768,512]{1,0:T(8,128)(2,1)S(1)}, bf16[768,512]{1,0:T(8,128)(2,1)S(1)}, u32[]{:S(2)}, u32[]{:S(2)}) collective-permute-start(bf16[768,512]{1,0:T(8,128)(2,1)S(1)} %copy-done.3), channel_id=1, source_target_pairs={{0,64},{64,128},{128,192},{192,0},{1,65},{65,129},{129,193},{193,1... | collective-permute-start | bytes 2359304 | tf_op jit(solution)/shard_map/ppermute | solution.py:15
  127.4 19.8 %collective-permute-start.6 = (bf16[768,512]{1,0:T(8,128)(2,1)S(1)}, bf16[768,512]{1,0:T(8,128)(2,1)S(1)}, u32[]{:S(2)}, u32[]{:S(2)}) collective-permute-start(bf16[768,512]{1,0:T(8,128)(2,1)S(1)} %copy-done.3), channel_id=1, source_target_pairs={{0,192},{64,0},{128,64},{192,128},{1,193},{65,1},{129,65},{193,129... | collective-permute-start | bytes 2359304 | tf_op jit(solution)/shard_map/ppermute | solution.py:15
  127.9 35.5 %collective-permute-start.7 = (bf16[768,512]{1,0:T(8,128)(2,1)S(1)}, bf16[768,512]{1,0:T(8,128)(2,1)}, u32[]{:S(2)}, u32[]{:S(2)}) collective-permute-start(bf16[768,512]{1,0:T(8,128)(2,1)S(1)} %copy-done.3), channel_id=1, source_target_pairs={{0,128},{64,192},{128,0},{192,64},{1,129},{65,193},{129,1},{193,65... | collective-permute-start | bytes 2359304 | tf_op jit(solution)/shard_map/ppermute | solution.py:15
  130.3 5.1 %collective-permute-start.18 = (bf16[128,2048]{1,0:T(8,128)(2,1)}, bf16[128,2048]{1,0:T(8,128)(2,1)}, u32[]{:S(2)}, u32[]{:S(2)}) collective-permute-start(bf16[128,2048]{1,0:T(8,128)(2,1)} %collective-permute-done.12.refs_4_), channel_id=1, source_target_pairs={{0,2},{2,0},{4,6},{6,4},{8,10},{10,8},{12,14},{14,12},{16,18},{18,... | collective-permute-start | bytes 1572872 | tf_op jit(solution)/shard_map/ppermute | solution.py:27
  131.9 3.5 %collective-permute-start.19 = (bf16[128,2048]{1,0:T(8,128)(2,1)}, bf16[128,2048]{1,0:T(8,128)(2,1)}, u32[]{:S(2)}, u32[]{:S(2)}) collective-permute-start(bf16[128,2048]{1,0:T(8,128)(2,1)} %collective-permute-done.13.refs_5_), channel_id=1, source_target_pairs={{0,2},{2,0},{4,6},{6,4},{8,10},{10,8},{12,14},{14,12},{16,18},{18,... | collective-permute-start | bytes 1572872 | tf_op jit(solution)/shard_map/ppermute | solution.py:27
  (22 other events, 515.5 us)

commit v3 on v2

v3 whole, which is shorter than its diff:
```python
import jax
import jax.numpy as jnp
from jax import lax
from jax.experimental import pallas as pl
from jax.experimental.pallas import tpu as pltpu
from jax.sharding import PartitionSpec as P


epsilon = 1e-06
bf16, f32 = jnp.bfloat16, jnp.float32
SMEM = pl.BlockSpec(memory_space=pltpu.SMEM)


def row_shift(x, by):
    return lax.ppermute(x, "row", [(i, (i + by) % 4) for i in range(4)])


def feat_swap(x):
    return lax.ppermute(x, "feat", [(0, 1), (1, 0)])


def col_move(x, move):
    def target(c):
        a, z, k = move(c // 16, (c // 2) % 8, c % 2)
        return a * 16 + z * 2 + k

    return lax.ppermute(x, "col", [(c, target(c)) for c in range(32)])


def core_swap(x):
    return col_move(x, lambda a, z, k: (a, z, 1 - k))


def deep_shift(x, by):
    return col_move(x, lambda a, z, k: (a, (z + by) % 8, k))


def fold_lanes(x):
    return sum(x[:, i : i + 128] for i in range(0, x.shape[1], 128))


def to_row(x):
    return jnp.sum(x.T, axis=0, keepdims=True)


def column(row, copies):
    tall = jnp.broadcast_to(row, (128, row.shape[1])).T
    return jnp.concatenate([tall] * copies, axis=1)


def shape(dims, dtype):
    return jax.ShapeDtypeStruct(dims, dtype)


VMEM = pl.BlockSpec(memory_space=pltpu.VMEM)


def room(mib):
    return pltpu.CompilerParams(vmem_limit_bytes=mib << 20)


def near_core(*arrays):
    return tuple(pltpu.with_memory_space_constraint(a, pltpu.VMEM) for a in arrays)


def far_core(*arrays):
    return tuple(pltpu.with_memory_space_constraint(a, pltpu.HBM) for a in arrays)


def strip(a, width=512):
    return pl.BlockSpec((a.shape[0], width), lambda i: (0, i))


def whole(a):
    return pl.BlockSpec(a.shape, lambda i: (0,) * len(a.shape))


def cut(step, width=512):
    return pl.ds(pl.multiple_of(step * width, width), width)


def norm_kernel(deep, core, ps, pt, ts, tt, sums, quarter, *refs):
    held, squares = refs[:4], refs[4]
    step = pl.program_id(0)
    quarter[:, cut(step)] = ps[cut(deep[0] * 2 + core[0], 128)]

    @pl.when(step == 0)
    def _():
        squares[...] = jnp.zeros_like(squares)

    start = 0
    for ref, copy in zip((ps, pt, ts, tt), held):
        for row in range(0, ref.shape[0], 128):
            block = ref[row : row + 128]
            copy[row : row + 128, cut(step)] = block
            values = block.astype(f32)
            squares[start : start + 128] += fold_lanes(values * values)
            start += 128

    @pl.when(step == pl.num_programs(0) - 1)
    def _():
        sums[...] = to_row(squares[...])


def norms(deep, core, *features):
    return pl.pallas_call(
        norm_kernel,
        grid=(4,),
        out_shape=[pltpu.VMEM((1, 2560), f32), pltpu.VMEM((128, 2048), bf16)]
        + [pltpu.VMEM(a.shape, bf16) for a in features],
        in_specs=[SMEM] * 2 + [strip(a) for a in features],
        out_specs=[VMEM] * 6,
        scratch_shapes=[pltpu.VMEM((2560, 128), f32)],
        compiler_params=room(12),
        name="norms",
    )(deep, core, *far_core(*features))


def gram_kernel(ps, pt, ts, tt, student, teacher):
    def inner(left, right):
        return lax.dot_general(left, right[...], (((1,), (1,)), ((), ())), preferred_element_type=f32)

    rows = cut(pl.program_id(0), 256)
    student[rows] = inner(ts[rows], ps)
    teacher[rows] = inner(tt[rows], pt)


def grams(*features):
    return pl.pallas_call(
        gram_kernel,
        grid=(3,),
        out_shape=[pltpu.VMEM((768, 512), f32)] * 2,
        in_specs=[VMEM] * 4,
        out_specs=[VMEM] * 2,
        compiler_params=room(12),
        name="grams",
    )(*near_core(*features))


def inverse(total):
    return 1.0 / jnp.sqrt(total + epsilon)


def inverses(mine, other):
    invs = inverse(mine[...] + other[...])
    return invs[:, :512], invs[:, 512:1024], column(invs[:, 1024:1792], 1), column(invs[:, 1792:], 1)


def wide(x):
    return jnp.concatenate([x] * 4, axis=1)


def part_kernel(student, teacher, mine, other, out):
    inv_ps, inv_pt, inv_ts, inv_tt = inverses(mine, other)
    for row in range(0, 768, 64):
        rows = slice(row, row + 64)
        near = student[rows] * inv_ps * wide(inv_ts[rows])
        out[rows] = (near - teacher[rows] * inv_pt * wide(inv_tt[rows])).astype(bf16)


def part_of(*arrays):
    return pl.pallas_call(
        part_kernel,
        out_shape=pltpu.VMEM((768, 512), bf16),
        in_specs=[VMEM] * 4,
        out_specs=VMEM,
        compiler_params=room(12),
        name="part",
    )(*near_core(*arrays))


def mismatch_kernel(student, teacher, mine, other, partner, doubled, weighted, loss, sides):
    inv_ps, inv_pt, inv_ts, inv_tt = inverses(mine, other)
    losses = jnp.zeros((1, 512), f32)
    products = jnp.zeros((1, 512), f32)
    for row in range(0, 768, 128):
        rows = slice(row, row + 128)
        scale = wide(inv_ts[rows])
        near = student[rows] * inv_ps * scale
        part = near - teacher[rows] * inv_pt * wide(inv_tt[rows])
        mismatch = part + partner[rows].astype(f32)
        twice = 2.0 * mismatch
        doubled[rows] = (twice * inv_ps).astype(bf16)
        weighted[:, rows] = (twice * scale).astype(bf16).T
        product = twice * near
        losses += jnp.sum(mismatch * mismatch, axis=0, keepdims=True)
        products += jnp.sum(product, axis=0, keepdims=True)
        sides[:, 512 + row : 640 + row] = to_row(fold_lanes(product))
    loss[...] = losses
    sides[:, :512] = products


def mismatch_of(*arrays):
    return pl.pallas_call(
        mismatch_kernel,
        out_shape=[
            pltpu.VMEM((768, 512), bf16),
            pltpu.VMEM((512, 768), bf16),
            pltpu.VMEM((1, 512), f32),
            pltpu.VMEM((1, 1280), f32),
        ],
        in_specs=[VMEM] * 5,
        out_specs=[VMEM] * 4,
        compiler_params=room(12),
        name="mismatch",
    )(*near_core(*arrays))


def pick(weighted, core, ts, step):
    return jnp.dot(weighted[:, core].reshape(256, 768), ts[:, cut(step)], preferred_element_type=f32)


def away_kernel(core, weighted, ts, away):
    step = pl.program_id(0)
    away[:, cut(step)] = pick(weighted, 1 - core[0], ts, step).astype(bf16)


def away_of(core, *arrays):
    return pl.pallas_call(
        away_kernel,
        grid=(4,),
        out_shape=pltpu.VMEM((256, 2048), bf16),
        in_specs=[SMEM] + [VMEM] * 2,
        out_specs=VMEM,
        compiler_params=room(12),
        name="away",
    )(core, *near_core(*arrays))


def join_kernel(core, weighted, ts, away, mine, other, out):
    step = pl.program_id(0)

    @pl.when(step < 4)
    def _():
        total = pick(weighted, core[0], ts, step) + away[:, cut(step)].astype(f32)
        out[...] = total.astype(bf16).reshape(16, 16, 512)

    @pl.when(step == 4)
    def _():
        stats = mine[...] + other[...]
        lane = lax.broadcasted_iota(jnp.int32, (512, 128), 1)
        tile = jnp.zeros((512, 128), f32)
        for row in range(2):
            total = column(stats[row : row + 1], 1)
            high = total.astype(bf16).astype(f32)
            tile = jnp.where(lane == 2 * row, high, jnp.where(lane == 2 * row + 1, total - high, tile))
        tile = tile.reshape(16, 2, 16, 128)
        out[:, :, :128] = jnp.where(core[0] == 0, tile[:, 0], tile[:, 1]).astype(bf16)


def join_of(core, *arrays):
    return pl.pallas_call(
        join_kernel,
        grid=(5,),
        out_shape=shape((16, 16, 2176), bf16),
        in_specs=[SMEM] + [VMEM] * 5,
        out_specs=pl.BlockSpec((16, 16, 512), lambda i: (0, 0, i)),
        compiler_params=room(12),
        name="join",
    )(core, *near_core(*arrays))


def final_kernel(spread, ps, inverses, loss, out):
    def total(lanes):
        return sum(spread[i, :, lanes].astype(f32) for i in range(16))

    stats = total(slice(2048, 2176))
    along = stats[:, 2:3] + stats[:, 3:4]
    for lane in range(0, 2048, 512):
        lanes = slice(lane, lane + 512)
        unit = ps[:, lanes].astype(f32) * inverses[...]
        out[:, lanes] = ((total(lanes) - unit * along) * inverses[...]).astype(bf16)
    turned = jnp.concatenate([stats, jnp.zeros((112, 128), f32)], axis=0).T
    loss[...] = (turned[0:1] + turned[1:2])[:, :16]


def final(*arrays):
    return pl.pallas_call(
        final_kernel,
        out_shape=[shape((1, 16), f32), shape((16, 2048), bf16)],
        in_specs=[VMEM] * 3,
        out_specs=[VMEM] * 2,
        compiler_params=room(12),
        name="final",
    )(*near_core(*arrays))


def token_kernel(deep, core, d0, dl, dr, do, ps, *refs):
    pieces, (ts, mine, other, a0, a1, a2, a3, out, work, twice) = refs[:12], refs[12:]
    deep, core = deep[0], core[0]

    @pl.when(pl.program_id(0) == 0)
    def _():
        for i, ref in enumerate((d0, dl, dr, do)):
            twice[:, i * 512 : i * 512 + 512] = ref[...]

    work[:512] = ps[...]
    for order, (a, b) in enumerate(((deep, core), (1 - deep, core), (deep, 1 - core), (1 - deep, 1 - core))):
        for side in range(3):
            start = pl.multiple_of(512 * side + 512 + (a * 2 + b) * 128, 128)
            work[pl.ds(start, 128)] = pieces[order * 3 + side][...]
    total = jnp.dot(twice[...], work[...], preferred_element_type=f32)
    inv_ts = inverse(mine[...] + other[...])[:, 1024:1792]
    along = a0[...] + a1[...] + a2[...] + a3[...]
    copies = ts.shape[1] // 128
    out[...] = (total * column(inv_ts, copies) - ts[...].astype(f32) * column(inv_ts * inv_ts * along, copies)).astype(bf16)


def token_grad(deep, core, doubled, ps, pieces, ts, mine, other, along):
    return pl.pallas_call(
        token_kernel,
        grid=(4,),
        out_shape=shape(ts.shape, bf16),
        in_specs=[SMEM] * 2
        + [whole(a) for a in doubled]
        + [strip(a) for a in (ps, *pieces, ts)]
        + [whole(a) for a in (mine, other, *along)],
        out_specs=strip(ts),
        scratch_shapes=[pltpu.VMEM((2048, 512), bf16), pltpu.VMEM((768, 2048), bf16)],
        name="tokens",
    )(deep, core, *far_core(*doubled, ps, *pieces, ts), mine, other, *along)


def local(panel_student, panel_teacher, tokens_student, tokens_teacher):
    col = lax.axis_index("col")
    deep, core = (col // 2) % 2, col % 2
    parity, index = deep.astype(jnp.int32)[None], core.astype(jnp.int32)[None]
    features = (panel_student, panel_teacher, tokens_student, tokens_teacher)

    mine, quarter, *held = norms(parity, index, *features)
    other = feat_swap(mine)
    student, teacher = grams(*held)
    part = part_of(student, teacher, mine, other)
    partner = feat_swap(part)

    left = row_shift(quarter, 1)
    right = row_shift(quarter, 3)
    far = row_shift(quarter, 2)
    first = (left, right, far)
    second = (deep_shift(left, 1), deep_shift(right, 7), deep_shift(far, 1))
    third = tuple(core_swap(a) for a in first)
    fourth = tuple(core_swap(a) for a in second)
    pieces = first + second + third + fourth

    doubled, weighted, loss, sides = mismatch_of(student, teacher, mine, other, partner)
    gathered = (doubled, row_shift(doubled, 1), row_shift(doubled, 3), row_shift(doubled, 2))
    weighted = weighted.reshape(16, 2, 16, 768)
    away = away_of(index, weighted, held[2])
    away = core_swap(away)

    sides += feat_swap(sides)
    stats = jnp.concatenate([loss, sides[:, :512]], axis=0)
    stats_other = core_swap(stats)
    along = sides[:, 512:]
    along = (along,) + tuple(row_shift(along, i) for i in (1, 2, 3))

    joined = join_of(index, weighted, held[2], away, stats, stats_other)
    groups = [[a * 16 + z * 2 + k for a in range(2) for z in range(8)] for k in range(2)]
    spread = lax.all_to_all(joined, "col", 0, 0, axis_index_groups=groups, tiled=True)

    grad_tokens = token_grad(parity, index, gathered, panel_student, pieces, tokens_student, mine, other, along)

    rows = lambda a: lax.dynamic_slice_in_dim(a, col * 16, 16, 0)
    inv_rows = inverse(rows(mine[0]) + rows(other[0]))[:, None]
    row_loss, grad_panel = final(spread, rows(panel_student), inv_rows)
    return (row_loss.reshape(16), grad_panel, grad_tokens)


def solution(mesh):
    placed = (P("row", "feat"), P("row", "feat"), P("col", "feat"), P("col", "feat"))
    return jax.shard_map(
        local,
        mesh=mesh,
        in_specs=placed,
        out_specs=(P(("row", "col")), P(("row", "col"), "feat"), P("col", "feat")),
        check_vma=False,
    )
```

time: 180 us -> 157 us (0.87)
  Pallas kernels: 47.1 us -> 29.1 us
  local copies, waits for them, and re-layouts: 8.84 us -> 2.46 us
  waiting for transfers between devices: 88.8 us -> 92 us
    pallas_call x5, Pallas kernels: 27.7 us -> 13.1 us  [the longest x1 6.07 us: norms(): pl.pallas_call(norm_kernel, grid=(4,), out_shape=[pltpu.VMEM((1, 2560), f...]
    unnamed x44 -> x30, local copies, waits for them, and re-layouts: 5.61 us -> 1.53 us
    pallas_call x1, Pallas kernels: 5.2 us -> 3.08 us  [join_of(): pl.pallas_call(join_kernel, grid=(5,), out_shape=shape((16, 16, 2176), bf...]
  transfers between devices with their start and end apart: 24 -> 24, of which waited for: 10 -> 11; matrix products, arithmetic and copies ran while one was open for 3% -> 1% of each run, Pallas kernels for 14% -> 12%
where the time goes in v3:
time: 157 us
  waiting for transfers between devices  92 us (59%)
  starting transfers between devices  32.1 us (20%)
  Pallas kernels  29.1 us (19%)
  local copies, waits for them, and re-layouts  2.46 us (2%)
    ppermute x9, waiting for transfers between devices, row_shift(): return lax.ppermute(x, 'row', [(i, (i + by) % 4) for i in range(4)])  37 us
    ppermute x11, waiting for transfers between devices, col_move(): return lax.ppermute(x, 'col', [(c, target(c)) for c in range(32)])  33.2 us
    ppermute x3, waiting for transfers between devices, feat_swap(): return lax.ppermute(x, 'feat', [(0, 1), (1, 0)])  21.8 us
    ppermute x9, starting transfers between devices, row_shift(): return lax.ppermute(x, 'row', [(i, (i + by) % 4) for i in range(4)])  12.8 us
    pallas_call x1, Pallas kernels, token_grad(): pl.pallas_call(token_kernel, grid=(4,), out_shape=shape(ts.shape, bf16),...  12.1 us
    all_to_all x1, starting transfers between devices, local(): lax.all_to_all(joined, 'col', 0, 0, axis_index_groups=groups, tiled=True)  8.6 us
    pallas_call x1, Pallas kernels, norms(): pl.pallas_call(norm_kernel, grid=(4,), out_shape=[pltpu.VMEM((1, 2560), f...  6.07 us
    ppermute x11, starting transfers between devices, col_move(): return lax.ppermute(x, 'col', [(c, target(c)) for c in range(32)])  5.59 us
  transfers between devices with their start and end apart: 24, of which 11 were waited for; matrix products, arithmetic and copies ran while one was open for 1% of the time, Pallas kernels for 12%

profile of v3, /device:TPU:8, one launch (start us, length us, event | category | flops | bytes accessed | tf_op | source)
XLA Modules:
  0.0 156.6 jit_solution(7287083596700216207)
XLA Ops:
  0.7 6.1 %norms.1 = (f32[1,2560]{1,0:T(1,128)S(1)}, bf16[128,2048]{1,0:T(8,128)(2,1)S(1)}, bf16[512,2048]{1,0:T(8,128)(2,1)S(1)}, bf16[512,2048]{1,0:T(8,128)(2,1)S(1)}, ...) custom-call(s32[1]{0:T(128)} %bitcast.1.deep, s32[1]{0:T(128)} %bitcast.core, bf16[512,2048]{1,0:T(8,128)(2,1)} %ps.3, ...), custom_call_target="tpu_custom_call" | custom-call | tf_op jit(solution)/shard_map/norms/pallas_call | solution.py:106
  6.8 3.1 %collective-permute-start = (f32[1,2560]{1,0:T(1,128)S(1)}, f32[1,2560]{1,0:T(1,128)S(1)}, u32[]{:S(2)}, u32[]{:S(2)}) collective-permute-start(f32[1,2560]{1,0:T(1,128)S(1)} %get-tuple-element.23.mine.refs_13_), channel_id=1, source_target_pairs={{0,1},{1,0},{2,3},{3,2},{4,5},{5,4},{6,7},{7,6},{8,9},{9,8},{10,11... | collective-permute-start | bytes 30728 | tf_op jit(solution)/shard_map/ppermute | solution.py:19
  9.9 3.9 %grams.1 = (f32[768,512]{1,0:T(8,128)S(1)}, f32[768,512]{1,0:T(8,128)S(1)}) custom-call(bf16[512,2048]{1,0:T(8,128)(2,1)S(1)} %get-tuple-element.17.ps, bf16[512,2048]{1,0:T(8,128)(2,1)S(1)} %get-tuple-element.18.pt, bf16[768,2048]{1,0:T(8,128)(2,1)S(1)} %get-tuple-element.19.ts, bf16[768,2048]{1,0:T(8,128)(2,1)S(1)} %get-tuple-element.20.tt), custom_call_target="tpu_custom_call" | custom-call | tf_op jit(solution)/shard_map/grams/pallas_call | solution.py:129
  14.2 1.4 collective-permute-start.1
  15.6 19.2 %collective-permute-done.1.partner = bf16[768,512]{1,0:T(8,128)(2,1)S(1)} collective-permute-done((bf16[768,512]{1,0:T(8,128)(2,1)S(1)}, bf16[768,512]{1,0:T(8,128)(2,1)S(1)}, u32[]{:S(2)}, u32[]{:S(2)}) %collective-permute-start.1) | collective-permute-done | bytes 786464 | tf_op jit(solution)/shard_map/ppermute | solution.py:19
  36.0 1.5 away.1
  38.2 1.6 %collective-permute-start.8 = (bf16[128,2048]{1,0:T(8,128)(2,1)S(1)}, bf16[128,2048]{1,0:T(8,128)(2,1)S(1)}, u32[]{:S(2)}, u32[]{:S(2)}) collective-permute-start(bf16[128,2048]{1,0:T(8,128)(2,1)S(1)} %get-tuple-element.30), channel_id=1, source_target_pairs={{0,64},{64,128},{128,192},{192,0},{1,65},{65,129},{129,193},{193,1... | collective-permute-start | bytes 1572872 | tf_op jit(solution)/shard_map/ppermute | solution.py:15
  40.3 2.6 %collective-permute-done.3 = f32[1,1280]{1,0:T(1,128)S(1)} collective-permute-done((f32[1,1280]{1,0:T(1,128)S(1)}, f32[1,1280]{1,0:T(1,128)S(1)}, u32[]{:S(2)}, u32[]{:S(2)}) %collective-permute-start.3) | collective-permute-done | bytes 5152 | tf_op jit(solution)/shard_map/ppermute | solution.py:19
  44.2 3.1 %join.1 = bf16[16,16,2176]{2,1,0:T(8,128)(2,1)} custom-call(s32[1]{0:T(128)} %bitcast.core, bf16[16,2,16,768]{3,2,1,0:T(8,128)(2,1)S(1)} %bitcast.7, bf16[768,2048]{1,0:T(8,128)(2,1)S(1)} %get-tuple-element.19.ts, bf16[256,2048]{1,0:T(8,128)(2,1)S(1)} %collective-permute-done.2.away, f32[2,512]{1,0:T(2,128)S(1)} %pad_maximum_fusion.mine, ...), custom_call_target="tpu_custom_call" | custom-call | tf_op jit(solution)/shard_map/join/pallas_call | solution.py:252
  47.2 8.6 %all-to-all-start = ((bf16[16,16,2176]{2,1,0:T(8,128)(2,1)}), bf16[16,16,2176]{2,1,0:T(8,128)(2,1)S(1)}, u32[]{:S(2)}, u32[]{:S(2)}) async-start(bf16[16,16,2176]{2,1,0:T(8,128)(2,1)} %join.1), calls=%async_computation | async-start | bytes 2228224 | tf_op jit(solution)/shard_map/all_to_all | solution.py:359
  55.8 2.4 %collective-permute-start.10 = (bf16[128,2048]{1,0:T(8,128)(2,1)S(1)}, bf16[128,2048]{1,0:T(8,128)(2,1)S(1)}, u32[]{:S(2)}, u32[]{:S(2)}) collective-permute-start(bf16[128,2048]{1,0:T(8,128)(2,1)S(1)} %get-tuple-element.30), channel_id=1, source_target_pairs={{0,128},{64,192},{128,0},{192,64},{1,129},{65,193},{129,1},{193,65... | collective-permute-start | bytes 1572872 | tf_op jit(solution)/shard_map/ppermute | solution.py:15
  58.2 1.8 %collective-permute-start.11 = (bf16[128,2048]{1,0:T(8,128)(2,1)S(1)}, bf16[128,2048]{1,0:T(8,128)(2,1)S(1)}, u32[]{:S(2)}, u32[]{:S(2)}) collective-permute-start(bf16[128,2048]{1,0:T(8,128)(2,1)S(1)} %collective-permute-done.8.refs_0_), channel_id=1, source_target_pairs={{0,4},{2,6},{4,8},{6,10},{8,12},{10,14},{12,16},{14,18},{16,20},{1... | collective-permute-start | bytes 1572872 | tf_op jit(solution)/shard_map/ppermute | solution.py:27
  60.1 1.4 collective-permute-start.12
  61.5 3.4 %collective-permute-start.21 = (f32[1,768]{1,0:T(1,128)S(1)}, f32[1,768]{1,0:T(1,128)S(1)}, u32[]{:S(2)}, u32[]{:S(2)}) collective-permute-start(f32[1,768]{1,0:T(1,128)S(1)} %slice.9.refs_15_), channel_id=1, source_target_pairs={{0,128},{64,192},{128,0},{192,64},{1,129},{65,193},{129,1},{193,65... | collective-permute-start | bytes 9224 | tf_op jit(solution)/shard_map/ppermute | solution.py:15
  64.9 6.3 %collective-permute-done.10.refs_2_ = bf16[128,2048]{1,0:T(8,128)(2,1)S(1)} collective-permute-done((bf16[128,2048]{1,0:T(8,128)(2,1)S(1)}, bf16[128,2048]{1,0:T(8,128)(2,1)S(1)}, u32[]{:S(2)}, u32[]{:S(2)}) %collective-permute-start.10) | collective-permute-done | bytes 524320 | tf_op jit(solution)/shard_map/ppermute | solution.py:15
  71.7 1.6 collective-permute-start.13
  73.3 1.5 collective-permute-done.22.refs_18_
  74.8 21.0 %collective-permute-done.11.refs_3_ = bf16[128,2048]{1,0:T(8,128)(2,1)S(1)} collective-permute-done((bf16[128,2048]{1,0:T(8,128)(2,1)S(1)}, bf16[128,2048]{1,0:T(8,128)(2,1)S(1)}, u32[]{:S(2)}, u32[]{:S(2)}) %collective-permute-start.11) | collective-permute-done | bytes 524320 | tf_op jit(solution)/shard_map/ppermute | solution.py:27
  96.3 9.8 %collective-permute-done.13.refs_5_ = bf16[128,2048]{1,0:T(8,128)(2,1)} collective-permute-done((bf16[128,2048]{1,0:T(8,128)(2,1)S(1)}, bf16[128,2048]{1,0:T(8,128)(2,1)}, u32[]{:S(2)}, u32[]{:S(2)}) %collective-permute-start.13) | collective-permute-done | bytes 524320 | tf_op jit(solution)/shard_map/ppermute | solution.py:27
  106.1 1.6 %collective-permute-start.5 = (bf16[768,512]{1,0:T(8,128)(2,1)S(1)}, bf16[768,512]{1,0:T(8,128)(2,1)S(1)}, u32[]{:S(2)}, u32[]{:S(2)}) collective-permute-start(bf16[768,512]{1,0:T(8,128)(2,1)S(1)} %get-tuple-element.29.d0), channel_id=1, source_target_pairs={{0,64},{64,128},{128,192},{192,0},{1,65},{65,129},{129,193},{193,1... | collective-permute-start | bytes 2359304 | tf_op jit(solution)/shard_map/ppermute | solution.py:15
  108.1 2.4 %collective-permute-start.7 = (bf16[768,512]{1,0:T(8,128)(2,1)S(1)}, bf16[768,512]{1,0:T(8,128)(2,1)}, u32[]{:S(2)}, u32[]{:S(2)}) collective-permute-start(bf16[768,512]{1,0:T(8,128)(2,1)S(1)} %get-tuple-element.29.d0), channel_id=1, source_target_pairs={{0,128},{64,192},{128,0},{192,64},{1,129},{65,193},{129,1},{193,65... | collective-permute-start | bytes 2359304 | tf_op jit(solution)/shard_map/ppermute | solution.py:15
  114.4 12.1 %collective-permute-done.5.dl = bf16[768,512]{1,0:T(8,128)(2,1)S(1)} collective-permute-done((bf16[768,512]{1,0:T(8,128)(2,1)S(1)}, bf16[768,512]{1,0:T(8,128)(2,1)S(1)}, u32[]{:S(2)}, u32[]{:S(2)}) %collective-permute-start.5) | collective-permute-done | bytes 786464 | tf_op jit(solution)/shard_map/ppermute | solution.py:15
  127.5 16.2 %collective-permute-done.7.do = bf16[768,512]{1,0:T(8,128)(2,1)} collective-permute-done((bf16[768,512]{1,0:T(8,128)(2,1)S(1)}, bf16[768,512]{1,0:T(8,128)(2,1)}, u32[]{:S(2)}, u32[]{:S(2)}) %collective-permute-start.7) | collective-permute-done | bytes 786464 | tf_op jit(solution)/shard_map/ppermute | solution.py:15
  143.7 12.1 %tokens.1 = bf16[768,2048]{1,0:T(8,128)(2,1)} custom-call(s32[1]{0:T(128)} %bitcast.1.deep, s32[1]{0:T(128)} %bitcast.core, bf16[768,512]{1,0:T(8,128)(2,1)} %copy-done, bf16[768,512]{1,0:T(8,128)(2,1)} %copy-done.3, bf16[768,512]{1,0:T(8,128)(2,1)} %collective-permute-done.6.dr, bf16[768,512]{1,0:T(8,128)(2,1)} %collective-permute-done.7.do, ...), custom_call_target="tpu_custom_call" | custom-call | tf_op jit(solution)/shard_map/tokens/pallas_call | solution.py:310
  (69 shorter events, 11.2 us)
Async XLA Ops:
  6.8 7.0 %collective-permute-start = (f32[1,2560]{1,0:T(1,128)S(1)}, f32[1,2560]{1,0:T(1,128)S(1)}, u32[]{:S(2)}, u32[]{:S(2)}) collective-permute-start(f32[1,2560]{1,0:T(1,128)S(1)} %get-tuple-element.23.mine.refs_13_), channel_id=1, source_target_pairs={{0,1},{1,0},{2,3},{3,2},{4,5},{5,4},{6,7},{7,6},{8,9},{9,8},{10,11... | collective-permute-start | bytes 30728 | tf_op jit(solution)/shard_map/ppermute | solution.py:19
  14.2 20.6 %collective-permute-start.1 = (bf16[768,512]{1,0:T(8,128)(2,1)S(1)}, bf16[768,512]{1,0:T(8,128)(2,1)S(1)}, u32[]{:S(2)}, u32[]{:S(2)}) collective-permute-start(bf16[768,512]{1,0:T(8,128)(2,1)S(1)} %part.1), channel_id=1, source_target_pairs={{0,1},{1,0},{2,3},{3,2},{4,5},{5,4},{6,7},{7,6},{8,9},{9,8},{10,11... | collective-permute-start | bytes 2359304 | tf_op jit(solution)/shard_map/ppermute | solution.py:19
  37.6 6.6 %collective-permute-start.2 = (bf16[256,2048]{1,0:T(8,128)(2,1)S(1)}, bf16[256,2048]{1,0:T(8,128)(2,1)S(1)}, u32[]{:S(2)}, u32[]{:S(2)}) collective-permute-start(bf16[256,2048]{1,0:T(8,128)(2,1)S(1)} %away.1), channel_id=1, source_target_pairs={{0,2},{2,0},{4,6},{6,4},{8,10},{10,8},{12,14},{14,12},{16,18},{18,... | collective-permute-start | bytes 3145736 | tf_op jit(solution)/shard_map/ppermute | solution.py:27
  37.7 5.2 %collective-permute-start.3 = (f32[1,1280]{1,0:T(1,128)S(1)}, f32[1,1280]{1,0:T(1,128)S(1)}, u32[]{:S(2)}, u32[]{:S(2)}) collective-permute-start(f32[1,1280]{1,0:T(1,128)S(1)} %get-tuple-element.26), channel_id=1, source_target_pairs={{0,1},{1,0},{2,3},{3,2},{4,5},{5,4},{6,7},{7,6},{8,9},{9,8},{10,11... | collective-permute-start | bytes 15368 | tf_op jit(solution)/shard_map/ppermute | solution.py:19
  38.2 20.0 %collective-permute-start.8 = (bf16[128,2048]{1,0:T(8,128)(2,1)S(1)}, bf16[128,2048]{1,0:T(8,128)(2,1)S(1)}, u32[]{:S(2)}, u32[]{:S(2)}) collective-permute-start(bf16[128,2048]{1,0:T(8,128)(2,1)S(1)} %get-tuple-element.30), channel_id=1, source_target_pairs={{0,64},{64,128},{128,192},{192,0},{1,65},{65,129},{129,193},{193,1... | collective-permute-start | bytes 1572872 | tf_op jit(solution)/shard_map/ppermute | solution.py:15
  39.8 20.3 %collective-permute-start.9 = (bf16[128,2048]{1,0:T(8,128)(2,1)S(1)}, bf16[128,2048]{1,0:T(8,128)(2,1)}, u32[]{:S(2)}, u32[]{:S(2)}) collective-permute-start(bf16[128,2048]{1,0:T(8,128)(2,1)S(1)} %get-tuple-element.30), channel_id=1, source_target_pairs={{0,192},{64,0},{128,64},{192,128},{1,193},{65,1},{129,65},{193,129... | collective-permute-start | bytes 1572872 | tf_op jit(solution)/shard_map/ppermute | solution.py:15
  42.9 1.3 collective-permute-start.4
  47.2 108.5 %all-to-all-start = ((bf16[16,16,2176]{2,1,0:T(8,128)(2,1)}), bf16[16,16,2176]{2,1,0:T(8,128)(2,1)S(1)}, u32[]{:S(2)}, u32[]{:S(2)}) async-start(bf16[16,16,2176]{2,1,0:T(8,128)(2,1)} %join.1), calls=%async_computation | async-start | bytes 2228224 | tf_op jit(solution)/shard_map/all_to_all | solution.py:359
  55.8 15.3 %collective-permute-start.10 = (bf16[128,2048]{1,0:T(8,128)(2,1)S(1)}, bf16[128,2048]{1,0:T(8,128)(2,1)S(1)}, u32[]{:S(2)}, u32[]{:S(2)}) collective-permute-start(bf16[128,2048]{1,0:T(8,128)(2,1)S(1)} %get-tuple-element.30), channel_id=1, source_target_pairs={{0,128},{64,192},{128,0},{192,64},{1,129},{65,193},{129,1},{193,65... | collective-permute-start | bytes 1572872 | tf_op jit(solution)/shard_map/ppermute | solution.py:15
  58.2 37.5 %collective-permute-start.11 = (bf16[128,2048]{1,0:T(8,128)(2,1)S(1)}, bf16[128,2048]{1,0:T(8,128)(2,1)S(1)}, u32[]{:S(2)}, u32[]{:S(2)}) collective-permute-start(bf16[128,2048]{1,0:T(8,128)(2,1)S(1)} %collective-permute-done.8.refs_0_), channel_id=1, source_target_pairs={{0,4},{2,6},{4,8},{6,10},{8,12},{10,14},{12,16},{14,18},{16,20},{1... | collective-permute-start | bytes 1572872 | tf_op jit(solution)/shard_map/ppermute | solution.py:27
  60.1 35.7 %collective-permute-start.12 = (bf16[128,2048]{1,0:T(8,128)(2,1)}, bf16[128,2048]{1,0:T(8,128)(2,1)}, u32[]{:S(2)}, u32[]{:S(2)}) collective-permute-start(bf16[128,2048]{1,0:T(8,128)(2,1)} %collective-permute-done.9.refs_1_), channel_id=1, source_target_pairs={{0,28},{2,30},{4,0},{6,2},{8,4},{10,6},{12,8},{14,10},{16,12},{18,... | collective-permute-start | bytes 1572872 | tf_op jit(solution)/shard_map/ppermute | solution.py:27
  61.5 10.2 %collective-permute-start.20 = (f32[1,768]{1,0:T(1,128)S(1)}, f32[1,768]{1,0:T(1,128)S(1)}, u32[]{:S(2)}, u32[]{:S(2)}) collective-permute-start(f32[1,768]{1,0:T(1,128)S(1)} %slice.9.refs_15_), channel_id=1, source_target_pairs={{0,64},{64,128},{128,192},{192,0},{1,65},{65,129},{129,193},{193,1... | collective-permute-start | bytes 9224 | tf_op jit(solution)/shard_map/ppermute | solution.py:15
  61.5 11.8 %collective-permute-start.21 = (f32[1,768]{1,0:T(1,128)S(1)}, f32[1,768]{1,0:T(1,128)S(1)}, u32[]{:S(2)}, u32[]{:S(2)}) collective-permute-start(f32[1,768]{1,0:T(1,128)S(1)} %slice.9.refs_15_), channel_id=1, source_target_pairs={{0,128},{64,192},{128,0},{192,64},{1,129},{65,193},{129,1},{193,65... | collective-permute-start | bytes 9224 | tf_op jit(solution)/shard_map/ppermute | solution.py:15
  71.2 3.6 %collective-permute-start.22 = (f32[1,768]{1,0:T(1,128)S(1)}, f32[1,768]{1,0:T(1,128)S(1)}, u32[]{:S(2)}, u32[]{:S(2)}) collective-permute-start(f32[1,768]{1,0:T(1,128)S(1)} %slice.9.refs_15_), channel_id=1, source_target_pairs={{0,192},{64,0},{128,64},{192,128},{1,193},{65,1},{129,65},{193,129... | collective-permute-start | bytes 9224 | tf_op jit(solution)/shard_map/ppermute | solution.py:15
  71.7 34.4 %collective-permute-start.13 = (bf16[128,2048]{1,0:T(8,128)(2,1)S(1)}, bf16[128,2048]{1,0:T(8,128)(2,1)}, u32[]{:S(2)}, u32[]{:S(2)}) collective-permute-start(bf16[128,2048]{1,0:T(8,128)(2,1)S(1)} %collective-permute-done.10.refs_2_), channel_id=1, source_target_pairs={{0,4},{2,6},{4,8},{6,10},{8,12},{10,14},{12,16},{14,18},{16,20},{1... | collective-permute-start | bytes 1572872 | tf_op jit(solution)/shard_map/ppermute | solution.py:27
  73.3 34.4 %collective-permute-start.14 = (bf16[128,2048]{1,0:T(8,128)(2,1)S(1)}, bf16[128,2048]{1,0:T(8,128)(2,1)S(1)}, u32[]{:S(2)}, u32[]{:S(2)}) collective-permute-start(bf16[128,2048]{1,0:T(8,128)(2,1)S(1)} %collective-permute-done.8.refs_0_), channel_id=1, source_target_pairs={{0,2},{2,0},{4,6},{6,4},{8,10},{10,8},{12,14},{14,12},{16,18},{18,... | collective-permute-start | bytes 1572872 | tf_op jit(solution)/shard_map/ppermute | solution.py:27
  74.8 33.3 %collective-permute-start.15 = (bf16[128,2048]{1,0:T(8,128)(2,1)}, bf16[128,2048]{1,0:T(8,128)(2,1)S(1)}, u32[]{:S(2)}, u32[]{:S(2)}) collective-permute-start(bf16[128,2048]{1,0:T(8,128)(2,1)} %collective-permute-done.9.refs_1_), channel_id=1, source_target_pairs={{0,2},{2,0},{4,6},{6,4},{8,10},{10,8},{12,14},{14,12},{16,18},{18,... | collective-permute-start | bytes 1572872 | tf_op jit(solution)/shard_map/ppermute | solution.py:27
  95.7 14.8 %collective-permute-start.16 = (bf16[128,2048]{1,0:T(8,128)(2,1)S(1)}, bf16[128,2048]{1,0:T(8,128)(2,1)S(1)}, u32[]{:S(2)}, u32[]{:S(2)}) collective-permute-start(bf16[128,2048]{1,0:T(8,128)(2,1)S(1)} %collective-permute-done.10.refs_2_), channel_id=1, source_target_pairs={{0,2},{2,0},{4,6},{6,4},{8,10},{10,8},{12,14},{14,12},{16,18},{18,... | collective-permute-start | bytes 1572872 | tf_op jit(solution)/shard_map/ppermute | solution.py:27
  95.7 14.9 %collective-permute-start.17 = (bf16[128,2048]{1,0:T(8,128)(2,1)S(1)}, bf16[128,2048]{1,0:T(8,128)(2,1)S(1)}, u32[]{:S(2)}, u32[]{:S(2)}) collective-permute-start(bf16[128,2048]{1,0:T(8,128)(2,1)S(1)} %collective-permute-done.11.refs_3_), channel_id=1, source_target_pairs={{0,2},{2,0},{4,6},{6,4},{8,10},{10,8},{12,14},{14,12},{16,18},{18,... | collective-permute-start | bytes 1572872 | tf_op jit(solution)/shard_map/ppermute | solution.py:27
  106.1 20.4 %collective-permute-start.5 = (bf16[768,512]{1,0:T(8,128)(2,1)S(1)}, bf16[768,512]{1,0:T(8,128)(2,1)S(1)}, u32[]{:S(2)}, u32[]{:S(2)}) collective-permute-start(bf16[768,512]{1,0:T(8,128)(2,1)S(1)} %get-tuple-element.29.d0), channel_id=1, source_target_pairs={{0,64},{64,128},{128,192},{192,0},{1,65},{65,129},{129,193},{193,1... | collective-permute-start | bytes 2359304 | tf_op jit(solution)/shard_map/ppermute | solution.py:15
  107.7 19.8 %collective-permute-start.6 = (bf16[768,512]{1,0:T(8,128)(2,1)S(1)}, bf16[768,512]{1,0:T(8,128)(2,1)}, u32[]{:S(2)}, u32[]{:S(2)}) collective-permute-start(bf16[768,512]{1,0:T(8,128)(2,1)S(1)} %get-tuple-element.29.d0), channel_id=1, source_target_pairs={{0,192},{64,0},{128,64},{192,128},{1,193},{65,1},{129,65},{193,129... | collective-permute-start | bytes 2359304 | tf_op jit(solution)/shard_map/ppermute | solution.py:15
  108.1 35.5 %collective-permute-start.7 = (bf16[768,512]{1,0:T(8,128)(2,1)S(1)}, bf16[768,512]{1,0:T(8,128)(2,1)}, u32[]{:S(2)}, u32[]{:S(2)}) collective-permute-start(bf16[768,512]{1,0:T(8,128)(2,1)S(1)} %get-tuple-element.29.d0), channel_id=1, source_target_pairs={{0,128},{64,192},{128,0},{192,64},{1,129},{65,193},{129,1},{193,65... | collective-permute-start | bytes 2359304 | tf_op jit(solution)/shard_map/ppermute | solution.py:15
  110.5 2.6 %collective-permute-start.18 = (bf16[128,2048]{1,0:T(8,128)(2,1)}, bf16[128,2048]{1,0:T(8,128)(2,1)}, u32[]{:S(2)}, u32[]{:S(2)}) collective-permute-start(bf16[128,2048]{1,0:T(8,128)(2,1)} %collective-permute-done.12.refs_4_), channel_id=1, source_target_pairs={{0,2},{2,0},{4,6},{6,4},{8,10},{10,8},{12,14},{14,12},{16,18},{18,... | collective-permute-start | bytes 1572872 | tf_op jit(solution)/shard_map/ppermute | solution.py:27
  112.1 2.3 %collective-permute-start.19 = (bf16[128,2048]{1,0:T(8,128)(2,1)}, bf16[128,2048]{1,0:T(8,128)(2,1)}, u32[]{:S(2)}, u32[]{:S(2)}) collective-permute-start(bf16[128,2048]{1,0:T(8,128)(2,1)} %collective-permute-done.13.refs_5_), channel_id=1, source_target_pairs={{0,2},{2,0},{4,6},{6,4},{8,10},{10,8},{12,14},{14,12},{16,18},{18,... | collective-permute-start | bytes 1572872 | tf_op jit(solution)/shard_map/ppermute | solution.py:27
  (15 other events, 734.7 us)

commit v4 on v3

--- a/solution.py
+++ b/solution.py
@@ -31,6 +31,10 @@
     return col_move(x, lambda a, z, k: (a, z, 1 - k))
 
 
+def near_swap(x):
+    return col_move(x, lambda a, z, k: (1 - a, z, k))
+
+
 def deep_shift(x, by):
     return col_move(x, lambda a, z, k: (a, (z + by) % 8, k))
 
@@ -71,18 +75,15 @@
     return pl.BlockSpec((a.shape[0], width), lambda i: (0, i))
 
 
-def whole(a):
-    return pl.BlockSpec(a.shape, lambda i: (0,) * len(a.shape))
-
-
 def cut(step, width=512):
     return pl.ds(pl.multiple_of(step * width, width), width)
 
 
-def norm_kernel(deep, core, ps, pt, ts, tt, sums, quarter, *refs):
+def norm_kernel(deep, core, col, ps, pt, ts, tt, sums, quarter, few, *refs):
     held, squares = refs[:4], refs[4]
     step = pl.program_id(0)
     quarter[:, cut(step)] = ps[cut(deep[0] * 2 + core[0], 128)]
+    few[:, cut(step)] = ps[cut(col[0], 16)]
 
     @pl.when(step == 0)
     def _():
@@ -102,18 +103,18 @@
         sums[...] = to_row(squares[...])
 
 
-def norms(deep, core, *features):
+def norms(deep, core, col, *features):
     return pl.pallas_call(
         norm_kernel,
         grid=(4,),
-        out_shape=[pltpu.VMEM((1, 2560), f32), pltpu.VMEM((128, 2048), bf16)]
+        out_shape=[pltpu.VMEM((1, 2560), f32), pltpu.VMEM((128, 2048), bf16), pltpu.VMEM((16, 2048), bf16)]
         + [pltpu.VMEM(a.shape, bf16) for a in features],
-        in_specs=[SMEM] * 2 + [strip(a) for a in features],
-        out_specs=[VMEM] * 6,
+        in_specs=[SMEM] * 3 + [strip(a) for a in features],
+        out_specs=[VMEM] * 7,
         scratch_shapes=[pltpu.VMEM((2560, 128), f32)],
         compiler_params=room(12),
         name="norms",
-    )(deep, core, *far_core(*features))
+    )(deep, core, col, *far_core(*features))
 
 
 def gram_kernel(ps, pt, ts, tt, student, teacher):
@@ -169,7 +170,7 @@
     )(*near_core(*arrays))
 
 
-def mismatch_kernel(student, teacher, mine, other, partner, doubled, weighted, loss, sides):
+def mismatch_kernel(student, teacher, mine, other, partner, doubled, weighted, sides):
     inv_ps, inv_pt, inv_ts, inv_tt = inverses(mine, other)
     losses = jnp.zeros((1, 512), f32)
     products = jnp.zeros((1, 512), f32)
@@ -186,8 +187,8 @@
         losses += jnp.sum(mismatch * mismatch, axis=0, keepdims=True)
         products += jnp.sum(product, axis=0, keepdims=True)
         sides[:, 512 + row : 640 + row] = to_row(fold_lanes(product))
-    loss[...] = losses
     sides[:, :512] = products
+    sides[:, 1280:] = losses
 
 
 def mismatch_of(*arrays):
@@ -196,11 +197,10 @@
         out_shape=[
             pltpu.VMEM((768, 512), bf16),
             pltpu.VMEM((512, 768), bf16),
-            pltpu.VMEM((1, 512), f32),
-            pltpu.VMEM((1, 1280), f32),
+            pltpu.VMEM((1, 1792), f32),
         ],
         in_specs=[VMEM] * 5,
-        out_specs=[VMEM] * 4,
+        out_specs=[VMEM] * 3,
         compiler_params=room(12),
         name="mismatch",
     )(*near_core(*arrays))
@@ -240,8 +240,8 @@
         stats = mine[...] + other[...]
         lane = lax.broadcasted_iota(jnp.int32, (512, 128), 1)
         tile = jnp.zeros((512, 128), f32)
-        for row in range(2):
-            total = column(stats[row : row + 1], 1)
+        for row, part in enumerate((0.5 * stats[:, 1280:], stats[:, :512])):
+            total = column(part, 1)
             high = total.astype(bf16).astype(f32)
             tile = jnp.where(lane == 2 * row, high, jnp.where(lane == 2 * row + 1, total - high, tile))
         tile = tile.reshape(16, 2, 16, 128)
@@ -252,7 +252,7 @@
     return pl.pallas_call(
         join_kernel,
         grid=(5,),
-        out_shape=shape((16, 16, 2176), bf16),
+        out_shape=pltpu.HBM((16, 16, 2176), bf16),
         in_specs=[SMEM] + [VMEM] * 5,
         out_specs=pl.BlockSpec((16, 16, 512), lambda i: (0, 0, i)),
         compiler_params=room(12),
@@ -260,74 +260,91 @@
     )(core, *near_core(*arrays))
 
 
-def final_kernel(spread, ps, inverses, loss, out):
+def final_kernel(col, spread, few, mine, other, loss, out, tall):
     def total(lanes):
         return sum(spread[i, :, lanes].astype(f32) for i in range(16))
 
+    tall[...] = column(inverse(mine[:, :512] + other[:, :512]), 1)
+    inv_rows = wide(tall[cut(col[0], 16)])
     stats = total(slice(2048, 2176))
     along = stats[:, 2:3] + stats[:, 3:4]
     for lane in range(0, 2048, 512):
         lanes = slice(lane, lane + 512)
-        unit = ps[:, lanes].astype(f32) * inverses[...]
-        out[:, lanes] = ((total(lanes) - unit * along) * inverses[...]).astype(bf16)
+        unit = few[:, lanes].astype(f32) * inv_rows
+        out[:, lanes] = ((total(lanes) - unit * along) * inv_rows).astype(bf16)
     turned = jnp.concatenate([stats, jnp.zeros((112, 128), f32)], axis=0).T
     loss[...] = (turned[0:1] + turned[1:2])[:, :16]
 
 
-def final(*arrays):
+def final(col, *arrays):
     return pl.pallas_call(
         final_kernel,
         out_shape=[shape((1, 16), f32), shape((16, 2048), bf16)],
-        in_specs=[VMEM] * 3,
+        in_specs=[SMEM] + [VMEM] * 4,
         out_specs=[VMEM] * 2,
+        scratch_shapes=[pltpu.VMEM((512, 128), f32)],
         compiler_params=room(12),
         name="final",
-    )(*near_core(*arrays))
-
-
-def token_kernel(deep, core, d0, dl, dr, do, ps, *refs):
-    pieces, (ts, mine, other, a0, a1, a2, a3, out, work, twice) = refs[:12], refs[12:]
+    )(col, *near_core(*arrays))
+
+
+def own_kernel(doubled, ps, out):
+    out[:, cut(pl.program_id(0))] = jnp.dot(doubled[...], ps[...], preferred_element_type=f32)
+
+
+def own_grad(doubled, ps):
+    return pl.pallas_call(
+        own_kernel,
+        grid=(4,),
+        out_shape=pltpu.VMEM((768, 2048), f32),
+        in_specs=[VMEM, strip(ps)],
+        out_specs=VMEM,
+        compiler_params=room(12),
+        name="own",
+    )(*near_core(doubled), *far_core(ps))
+
+
+def token_kernel(deep, core, dl, dr, do, *refs):
+    pieces, (ts, own, mine, other, a0, a1, a2, a3, out, work, twice) = refs[:12], refs[12:]
     deep, core = deep[0], core[0]
-
-    @pl.when(pl.program_id(0) == 0)
-    def _():
-        for i, ref in enumerate((d0, dl, dr, do)):
+    step = pl.program_id(0)
+
+    @pl.when(step == 0)
+    def _():
+        for i, ref in enumerate((dl, dr, do)):
             twice[:, i * 512 : i * 512 + 512] = ref[...]
 
-    work[:512] = ps[...]
     for order, (a, b) in enumerate(((deep, core), (1 - deep, core), (deep, 1 - core), (1 - deep, 1 - core))):
         for side in range(3):
-            start = pl.multiple_of(512 * side + 512 + (a * 2 + b) * 128, 128)
-            work[pl.ds(start, 128)] = pieces[order * 3 + side][...]
-    total = jnp.dot(twice[...], work[...], preferred_element_type=f32)
+            start = pl.multiple_of(512 * side + (a * 2 + b) * 128, 128)
+            work[pl.ds(start, 128)] = pieces[order * 3 + side][:, cut(step)]
+    total = jnp.dot(twice[...], work[...], preferred_element_type=f32) + own[:, cut(step)]
     inv_ts = inverse(mine[...] + other[...])[:, 1024:1792]
-    along = a0[...] + a1[...] + a2[...] + a3[...]
-    copies = ts.shape[1] // 128
-    out[...] = (total * column(inv_ts, copies) - ts[...].astype(f32) * column(inv_ts * inv_ts * along, copies)).astype(bf16)
-
-
-def token_grad(deep, core, doubled, ps, pieces, ts, mine, other, along):
+    along = (a0[...] + a1[...] + a2[...] + a3[...])[:, 512:1280]
+    scale, shade = wide(column(inv_ts, 1)), wide(column(inv_ts * inv_ts * along, 1))
+    out[...] = (total * scale - ts[:, cut(step)].astype(f32) * shade).astype(bf16)
+
+
+def token_grad(deep, core, *arrays):
     return pl.pallas_call(
         token_kernel,
         grid=(4,),
-        out_shape=shape(ts.shape, bf16),
-        in_specs=[SMEM] * 2
-        + [whole(a) for a in doubled]
-        + [strip(a) for a in (ps, *pieces, ts)]
-        + [whole(a) for a in (mine, other, *along)],
-        out_specs=strip(ts),
-        scratch_shapes=[pltpu.VMEM((2048, 512), bf16), pltpu.VMEM((768, 2048), bf16)],
+        out_shape=shape((768, 2048), bf16),
+        in_specs=[SMEM] * 2 + [VMEM] * len(arrays),
+        out_specs=pl.BlockSpec((768, 512), lambda i: (0, i)),
+        scratch_shapes=[pltpu.VMEM((1536, 512), bf16), pltpu.VMEM((768, 1536), bf16)],
+        compiler_params=room(18),
         name="tokens",
-    )(deep, core, *far_core(*doubled, ps, *pieces, ts), mine, other, *along)
+    )(deep, core, *near_core(*arrays))
 
 
 def local(panel_student, panel_teacher, tokens_student, tokens_teacher):
     col = lax.axis_index("col")
-    deep, core = (col // 2) % 2, col % 2
-    parity, index = deep.astype(jnp.int32)[None], core.astype(jnp.int32)[None]
+    deep, core = (col // 16 + col // 2) % 2, col % 2
+    parity, index, place = (a.astype(jnp.int32)[None] for a in (deep, core, col))
     features = (panel_student, panel_teacher, tokens_student, tokens_teacher)
 
-    mine, quarter, *held = norms(parity, index, *features)
+    mine, quarter, few, *held = norms(parity, index, place, *features)
     other = feat_swap(mine)
     student, teacher = grams(*held)
     part = part_of(student, teacher, mine, other)
@@ -337,32 +354,29 @@
     right = row_shift(quarter, 3)
     far = row_shift(quarter, 2)
     first = (left, right, far)
-    second = (deep_shift(left, 1), deep_shift(right, 7), deep_shift(far, 1))
+    second = (deep_shift(left, 1), deep_shift(right, 7), near_swap(far))
     third = tuple(core_swap(a) for a in first)
     fourth = tuple(core_swap(a) for a in second)
     pieces = first + second + third + fourth
 
-    doubled, weighted, loss, sides = mismatch_of(student, teacher, mine, other, partner)
-    gathered = (doubled, row_shift(doubled, 1), row_shift(doubled, 3), row_shift(doubled, 2))
+    doubled, weighted, sides = mismatch_of(student, teacher, mine, other, partner)
+    gathered = (row_shift(doubled, 1), row_shift(doubled, 3), row_shift(doubled, 2))
     weighted = weighted.reshape(16, 2, 16, 768)
     away = away_of(index, weighted, held[2])
     away = core_swap(away)
 
     sides += feat_swap(sides)
-    stats = jnp.concatenate([loss, sides[:, :512]], axis=0)
-    stats_other = core_swap(stats)
-    along = sides[:, 512:]
-    along = (along,) + tuple(row_shift(along, i) for i in (1, 2, 3))
-
-    joined = join_of(index, weighted, held[2], away, stats, stats_other)
+    stats_other = core_swap(sides)
+    along = (sides,) + tuple(row_shift(sides, i) for i in (1, 2, 3))
+
+    joined = join_of(index, weighted, held[2], away, sides, stats_other)
     groups = [[a * 16 + z * 2 + k for a in range(2) for z in range(8)] for k in range(2)]
     spread = lax.all_to_all(joined, "col", 0, 0, axis_index_groups=groups, tiled=True)
 
-    grad_tokens = token_grad(parity, index, gathered, panel_student, pieces, tokens_student, mine, other, along)
-
-    rows = lambda a: lax.dynamic_slice_in_dim(a, col * 16, 16, 0)
-    inv_rows = inverse(rows(mine[0]) + rows(other[0]))[:, None]
-    row_loss, grad_panel = final(spread, rows(panel_student), inv_rows)
+    own = own_grad(doubled, panel_student)
+    grad_tokens = token_grad(parity, index, *gathered, *pieces, held[2], own, mine, other, *along)
+
+    row_loss, grad_panel = final(place, spread, few, mine, other)
     return (row_loss.reshape(16), grad_panel, grad_tokens)
 
 

time: 157 us -> 135 us (0.86); the launches traced: 157 us -> 132 us
  waiting for transfers between devices: 92 us -> 63.3 us
  starting transfers between devices: 32.1 us -> 34.7 us
  Pallas kernels: 29.1 us -> 31.4 us
    ppermute x11, waiting for transfers between devices: 33.2 us -> 12.6 us  [col_move(): return lax.ppermute(x, 'col', [(c, target(c)) for c in range(32)])]
    ppermute x9, waiting for transfers between devices: 37 us -> 29.1 us  [row_shift(): return lax.ppermute(x, 'row', [(i, (i + by) % 4) for i in range(4)])]
    ppermute x9, starting transfers between devices: 12.8 us -> 14.9 us  [row_shift(): return lax.ppermute(x, 'row', [(i, (i + by) % 4) for i in range(4)])]
    pallas_call x2 -> x3, Pallas kernels: 15.2 us -> 15.3 us  [the longest x1 8.36 us: token_grad(): pl.pallas_call(token_kernel, grid=(4,), out_shape=shape((768, 2048), bf16...]
  transfers between devices with their start and end apart: 24 -> 24, of which waited for: 11 -> 9; matrix products, arithmetic and copies ran while one was open for 1% -> 0% of each run, Pallas kernels for 12% -> 15%
where the time goes in v4:
time: 135 us; the launch traced here: 132 us
  waiting for transfers between devices  63.3 us (47%)
  starting transfers between devices  34.7 us (26%)
  Pallas kernels  31.4 us (23%)
  local copies, waits for them, and re-layouts  2.01 us (1%)
    ppermute x9, waiting for transfers between devices, row_shift(): return lax.ppermute(x, 'row', [(i, (i + by) % 4) for i in range(4)])  29.1 us
    ppermute x3, waiting for transfers between devices, feat_swap(): return lax.ppermute(x, 'feat', [(0, 1), (1, 0)])  21.5 us
    ppermute x9, starting transfers between devices, row_shift(): return lax.ppermute(x, 'row', [(i, (i + by) % 4) for i in range(4)])  14.9 us
    ppermute x11, waiting for transfers between devices, col_move(): return lax.ppermute(x, 'col', [(c, target(c)) for c in range(32)])  12.6 us
    all_to_all x1, starting transfers between devices, local(): lax.all_to_all(joined, 'col', 0, 0, axis_index_groups=groups, tiled=True)  8.64 us
    pallas_call x1, Pallas kernels, token_grad(): pl.pallas_call(token_kernel, grid=(4,), out_shape=shape((768, 2048), bf16...  8.36 us
    pallas_call x1, Pallas kernels, norms(): pl.pallas_call(norm_kernel, grid=(4,), out_shape=[pltpu.VMEM((1, 2560), f...  6.83 us
    ppermute x11, starting transfers between devices, col_move(): return lax.ppermute(x, 'col', [(c, target(c)) for c in range(32)])  6.13 us
  transfers between devices with their start and end apart: 24, of which 9 were waited for; matrix products, arithmetic and copies ran while one was open for 0% of the time, Pallas kernels for 15%

profile of v4, /device:TPU:8, one launch (start us, length us, event | category | flops | bytes accessed | tf_op | source)
XLA Modules:
  0.0 132.2 jit_solution(9033910148862008307)
XLA Ops:
  0.7 6.8 %norms.1 = (f32[1,2560]{1,0:T(1,128)S(1)}, bf16[128,2048]{1,0:T(8,128)(2,1)}, bf16[16,2048]{1,0:T(8,128)(2,1)S(1)}, bf16[512,2048]{1,0:T(8,128)(2,1)S(1)}, bf16[...) custom-call(s32[1]{0:T(128)} %bitcast.2.deep, s32[1]{0:T(128)} %bitcast.1.core, ...), custom_call_target="tpu_custom_call" | custom-call | tf_op jit(solution)/shard_map/norms/pallas_call | solution.py:107
  7.5 3.0 %collective-permute-start = (f32[1,2560]{1,0:T(1,128)S(1)}, f32[1,2560]{1,0:T(1,128)S(1)}, u32[]{:S(2)}, u32[]{:S(2)}) collective-permute-start(f32[1,2560]{1,0:T(1,128)S(1)} %get-tuple-element.23.mine.refs_14_), channel_id=1, source_target_pairs={{0,1},{1,0},{2,3},{3,2},{4,5},{5,4},{6,7},{7,6},{8,9},{9,8},{10,11... | collective-permute-start | bytes 30728 | tf_op jit(solution)/shard_map/ppermute | solution.py:19
  10.5 3.9 %grams.1 = (f32[768,512]{1,0:T(8,128)S(1)}, f32[768,512]{1,0:T(8,128)S(1)}) custom-call(bf16[512,2048]{1,0:T(8,128)(2,1)S(1)} %get-tuple-element.17.ps, bf16[512,2048]{1,0:T(8,128)(2,1)S(1)} %get-tuple-element.18.pt, bf16[768,2048]{1,0:T(8,128)(2,1)S(1)} %get-tuple-element.19.ts.refs_12_, bf16[768,2048]{1,0:T(8,128)(2,1)S(1)} %get-tuple-element.20.tt), custom_call_target="tpu_custom_call" | custom-call | tf_op jit(solution)/shard_map/grams/pallas_call | solution.py:130
  16.3 19.2 %collective-permute-done.1.partner = bf16[768,512]{1,0:T(8,128)(2,1)S(1)} collective-permute-done((bf16[768,512]{1,0:T(8,128)(2,1)S(1)}, bf16[768,512]{1,0:T(8,128)(2,1)S(1)}, u32[]{:S(2)}, u32[]{:S(2)}) %collective-permute-start.1) | collective-permute-done | bytes 786464 | tf_op jit(solution)/shard_map/ppermute | solution.py:19
  39.8 2.3 %collective-permute-start.10 = (bf16[128,2048]{1,0:T(8,128)(2,1)}, bf16[128,2048]{1,0:T(8,128)(2,1)}, u32[]{:S(2)}, u32[]{:S(2)}) collective-permute-start(bf16[128,2048]{1,0:T(8,128)(2,1)} %get-tuple-element.30), channel_id=1, source_target_pairs={{0,128},{64,192},{128,0},{192,64},{1,129},{65,193},{129,1},{193,65... | collective-permute-start | bytes 1572872 | tf_op jit(solution)/shard_map/ppermute | solution.py:15
  42.1 2.3 %collective-permute-done.3 = f32[1,1792]{1,0:T(1,128)S(1)} collective-permute-done((f32[1,1792]{1,0:T(1,128)S(1)}, f32[1,1792]{1,0:T(1,128)S(1)}, u32[]{:S(2)}, u32[]{:S(2)}) %collective-permute-start.3) | collective-permute-done | bytes 7200 | tf_op jit(solution)/shard_map/ppermute | solution.py:19
  45.7 3.1 %join.1 = bf16[16,16,2176]{2,1,0:T(8,128)(2,1)} custom-call(s32[1]{0:T(128)} %bitcast.1.core, bf16[16,2,16,768]{3,2,1,0:T(8,128)(2,1)S(1)} %bitcast.6, bf16[768,2048]{1,0:T(8,128)(2,1)S(1)} %get-tuple-element.19.ts.refs_12_, bf16[256,2048]{1,0:T(8,128)(2,1)S(1)} %collective-permute-done.2.away, f32[1,1792]{1,0:T(1,128)S(1)} %add.18.mine.refs_16_, ...), custom_call_target="tpu_custom_call" | custom-call | tf_op jit(solution)/shard_map/join/pallas_call | solution.py:252
  48.9 8.6 %all-to-all-start = ((bf16[16,16,2176]{2,1,0:T(8,128)(2,1)}), bf16[16,16,2176]{2,1,0:T(8,128)(2,1)}, u32[]{:S(2)}, u32[]{:S(2)}) async-start(bf16[16,16,2176]{2,1,0:T(8,128)(2,1)} %join.1), calls=%async_computation | async-start | bytes 2228224 | tf_op jit(solution)/shard_map/all_to_all | solution.py:374
  58.0 1.6 %collective-permute-start.8 = (bf16[128,2048]{1,0:T(8,128)(2,1)}, bf16[128,2048]{1,0:T(8,128)(2,1)S(1)}, u32[]{:S(2)}, u32[]{:S(2)}) collective-permute-start(bf16[128,2048]{1,0:T(8,128)(2,1)} %get-tuple-element.30), channel_id=1, source_target_pairs={{0,64},{64,128},{128,192},{192,0},{1,65},{65,129},{129,193},{193,1... | collective-permute-start | bytes 1572872 | tf_op jit(solution)/shard_map/ppermute | solution.py:15
  59.6 1.8 %collective-permute-start.13 = (bf16[128,2048]{1,0:T(8,128)(2,1)}, bf16[128,2048]{1,0:T(8,128)(2,1)S(1)}, u32[]{:S(2)}, u32[]{:S(2)}) collective-permute-start(bf16[128,2048]{1,0:T(8,128)(2,1)} %collective-permute-done.10.refs_2_), channel_id=1, source_target_pairs={{0,32},{2,34},{4,36},{6,38},{8,40},{10,42},{12,44},{14,46},{16,48}... | collective-permute-start | bytes 1572872 | tf_op jit(solution)/shard_map/ppermute | solution.py:27
  61.4 1.5 %collective-permute-start.22 = (f32[1,1792]{1,0:T(1,128)S(1)}, f32[1,1792]{1,0:T(1,128)S(1)}, u32[]{:S(2)}, u32[]{:S(2)}) collective-permute-start(f32[1,1792]{1,0:T(1,128)S(1)} %add.18.mine.refs_16_), channel_id=1, source_target_pairs={{0,192},{64,0},{128,64},{192,128},{1,193},{65,1},{129,65},{193,129... | collective-permute-start | bytes 21512 | tf_op jit(solution)/shard_map/ppermute | solution.py:15
  63.0 8.6 %collective-permute-done.9.refs_1_ = bf16[128,2048]{1,0:T(8,128)(2,1)S(1)} collective-permute-done((bf16[128,2048]{1,0:T(8,128)(2,1)}, bf16[128,2048]{1,0:T(8,128)(2,1)S(1)}, u32[]{:S(2)}, u32[]{:S(2)}) %collective-permute-start.9) | collective-permute-done | bytes 524320 | tf_op jit(solution)/shard_map/ppermute | solution.py:15
  71.6 3.5 %collective-permute-start.21 = (f32[1,1792]{1,0:T(1,128)S(1)}, f32[1,1792]{1,0:T(1,128)S(1)}, u32[]{:S(2)}, u32[]{:S(2)}) collective-permute-start(f32[1,1792]{1,0:T(1,128)S(1)} %add.18.mine.refs_16_), channel_id=1, source_target_pairs={{0,128},{64,192},{128,0},{192,64},{1,129},{65,193},{129,1},{193,65... | collective-permute-start | bytes 21512 | tf_op jit(solution)/shard_map/ppermute | solution.py:15
  75.2 1.5 %collective-permute-done.21.refs_18_ = f32[1,1792]{1,0:T(1,128)S(1)} collective-permute-done((f32[1,1792]{1,0:T(1,128)S(1)}, f32[1,1792]{1,0:T(1,128)S(1)}, u32[]{:S(2)}, u32[]{:S(2)}) %collective-permute-start.21) | collective-permute-done | bytes 7200 | tf_op jit(solution)/shard_map/ppermute | solution.py:15
  76.7 2.7 %collective-permute-start.12 = (bf16[128,2048]{1,0:T(8,128)(2,1)S(1)}, bf16[128,2048]{1,0:T(8,128)(2,1)S(1)}, u32[]{:S(2)}, u32[]{:S(2)}) collective-permute-start(bf16[128,2048]{1,0:T(8,128)(2,1)S(1)} %collective-permute-done.9.refs_1_), channel_id=1, source_target_pairs={{0,28},{2,30},{4,0},{6,2},{8,4},{10,6},{12,8},{14,10},{16,12},{18,... | collective-permute-start | bytes 1572872 | tf_op jit(solution)/shard_map/ppermute | solution.py:27
  80.3 2.7 %collective-permute-done.13.refs_5_ = bf16[128,2048]{1,0:T(8,128)(2,1)S(1)} collective-permute-done((bf16[128,2048]{1,0:T(8,128)(2,1)}, bf16[128,2048]{1,0:T(8,128)(2,1)S(1)}, u32[]{:S(2)}, u32[]{:S(2)}) %collective-permute-start.13) | collective-permute-done | bytes 524320 | tf_op jit(solution)/shard_map/ppermute | solution.py:27
  82.9 3.4 %collective-permute-start.7 = (bf16[768,512]{1,0:T(8,128)(2,1)}, bf16[768,512]{1,0:T(8,128)(2,1)S(1)}, u32[]{:S(2)}, u32[]{:S(2)}) collective-permute-start(bf16[768,512]{1,0:T(8,128)(2,1)} %copy-done), channel_id=1, source_target_pairs={{0,128},{64,192},{128,0},{192,64},{1,129},{65,193},{129,1},{193,65... | collective-permute-start | bytes 2359304 | tf_op jit(solution)/shard_map/ppermute | solution.py:15
  86.4 8.8 %collective-permute-done.12.refs_4_ = bf16[128,2048]{1,0:T(8,128)(2,1)S(1)} collective-permute-done((bf16[128,2048]{1,0:T(8,128)(2,1)S(1)}, bf16[128,2048]{1,0:T(8,128)(2,1)S(1)}, u32[]{:S(2)}, u32[]{:S(2)}) %collective-permute-start.12) | collective-permute-done | bytes 524320 | tf_op jit(solution)/shard_map/ppermute | solution.py:27
  95.6 1.6 %collective-permute-start.5 = (bf16[768,512]{1,0:T(8,128)(2,1)}, bf16[768,512]{1,0:T(8,128)(2,1)S(1)}, u32[]{:S(2)}, u32[]{:S(2)}) collective-permute-start(bf16[768,512]{1,0:T(8,128)(2,1)} %copy-done), channel_id=1, source_target_pairs={{0,64},{64,128},{128,192},{192,0},{1,65},{65,129},{129,193},{193,1... | collective-permute-start | bytes 2359304 | tf_op jit(solution)/shard_map/ppermute | solution.py:15
  98.8 3.9 %own.1.refs_13_ = f32[768,2048]{1,0:T(8,128)S(1)} custom-call(bf16[768,512]{1,0:T(8,128)(2,1)S(1)} %copy-done.1, bf16[512,2048]{1,0:T(8,128)(2,1)} %ps.3), custom_call_target="tpu_custom_call" | custom-call | tf_op jit(solution)/shard_map/own/pallas_call | solution.py:296
  102.7 2.4 %collective-permute-done.7.do = bf16[768,512]{1,0:T(8,128)(2,1)S(1)} collective-permute-done((bf16[768,512]{1,0:T(8,128)(2,1)}, bf16[768,512]{1,0:T(8,128)(2,1)S(1)}, u32[]{:S(2)}, u32[]{:S(2)}) %collective-permute-start.7) | collective-permute-done | bytes 786464 | tf_op jit(solution)/shard_map/ppermute | solution.py:15
  105.1 16.5 %collective-permute-done.6.dr = bf16[768,512]{1,0:T(8,128)(2,1)S(1)} collective-permute-done((bf16[768,512]{1,0:T(8,128)(2,1)}, bf16[768,512]{1,0:T(8,128)(2,1)S(1)}, u32[]{:S(2)}, u32[]{:S(2)}) %collective-permute-start.6) | collective-permute-done | bytes 786464 | tf_op jit(solution)/shard_map/ppermute | solution.py:15
  121.7 8.4 %tokens.1 = bf16[768,2048]{1,0:T(8,128)(2,1)} custom-call(s32[1]{0:T(128)} %bitcast.2.deep, s32[1]{0:T(128)} %bitcast.1.core, bf16[768,512]{1,0:T(8,128)(2,1)S(1)} %collective-permute-done.5.dl, bf16[768,512]{1,0:T(8,128)(2,1)S(1)} %collective-permute-done.6.dr, bf16[768,512]{1,0:T(8,128)(2,1)S(1)} %collective-permute-done.7.do, ...), custom_call_target="tpu_custom_call" | custom-call | tf_op jit(solution)/shard_map/tokens/pallas_call | solution.py:329
  130.0 2.1 %final.1 = (f32[1,16]{1,0:T(1,128)}, bf16[16,2048]{1,0:T(8,128)(2,1)}) custom-call(s32[1]{0:T(128)} %bitcast.col, bf16[16,16,2176]{2,1,0:T(8,128)(2,1)} %all-to-all-done.spread, bf16[16,2048]{1,0:T(8,128)(2,1)S(1)} %get-tuple-element.26.few, f32[1,2560]{1,0:T(1,128)S(1)} %get-tuple-element.23.mine.refs_14_, f32[1,2560]{1,0:T(1,128)S(1)} %collective-permute-done.other.refs_15_), custom_call_target="tpu_custom_call" | custom-call | tf_op jit(solution)/shard_map/final/pallas_call | solution.py:280
  (38 shorter events, 11.0 us)
Async XLA Ops:
  7.5 6.9 %collective-permute-start = (f32[1,2560]{1,0:T(1,128)S(1)}, f32[1,2560]{1,0:T(1,128)S(1)}, u32[]{:S(2)}, u32[]{:S(2)}) collective-permute-start(f32[1,2560]{1,0:T(1,128)S(1)} %get-tuple-element.23.mine.refs_14_), channel_id=1, source_target_pairs={{0,1},{1,0},{2,3},{3,2},{4,5},{5,4},{6,7},{7,6},{8,9},{9,8},{10,11... | collective-permute-start | bytes 30728 | tf_op jit(solution)/shard_map/ppermute | solution.py:19
  14.9 20.6 %collective-permute-start.1 = (bf16[768,512]{1,0:T(8,128)(2,1)S(1)}, bf16[768,512]{1,0:T(8,128)(2,1)S(1)}, u32[]{:S(2)}, u32[]{:S(2)}) collective-permute-start(bf16[768,512]{1,0:T(8,128)(2,1)S(1)} %part.1), channel_id=1, source_target_pairs={{0,1},{1,0},{2,3},{3,2},{4,5},{5,4},{6,7},{7,6},{8,9},{9,8},{10,11... | collective-permute-start | bytes 2359304 | tf_op jit(solution)/shard_map/ppermute | solution.py:19
  39.1 6.6 %collective-permute-start.2 = (bf16[256,2048]{1,0:T(8,128)(2,1)S(1)}, bf16[256,2048]{1,0:T(8,128)(2,1)S(1)}, u32[]{:S(2)}, u32[]{:S(2)}) collective-permute-start(bf16[256,2048]{1,0:T(8,128)(2,1)S(1)} %away.1), channel_id=1, source_target_pairs={{0,2},{2,0},{4,6},{6,4},{8,10},{10,8},{12,14},{14,12},{16,18},{18,... | collective-permute-start | bytes 3145736 | tf_op jit(solution)/shard_map/ppermute | solution.py:27
  39.2 5.2 %collective-permute-start.3 = (f32[1,1792]{1,0:T(1,128)S(1)}, f32[1,1792]{1,0:T(1,128)S(1)}, u32[]{:S(2)}, u32[]{:S(2)}) collective-permute-start(f32[1,1792]{1,0:T(1,128)S(1)} %get-tuple-element.25), channel_id=1, source_target_pairs={{0,1},{1,0},{2,3},{3,2},{4,5},{5,4},{6,7},{7,6},{8,9},{9,8},{10,11... | collective-permute-start | bytes 21512 | tf_op jit(solution)/shard_map/ppermute | solution.py:19
  39.8 19.8 %collective-permute-start.10 = (bf16[128,2048]{1,0:T(8,128)(2,1)}, bf16[128,2048]{1,0:T(8,128)(2,1)}, u32[]{:S(2)}, u32[]{:S(2)}) collective-permute-start(bf16[128,2048]{1,0:T(8,128)(2,1)} %get-tuple-element.30), channel_id=1, source_target_pairs={{0,128},{64,192},{128,0},{192,64},{1,129},{65,193},{129,1},{193,65... | collective-permute-start | bytes 1572872 | tf_op jit(solution)/shard_map/ppermute | solution.py:15
  44.5 1.3 collective-permute-start.4
  48.9 81.2 %all-to-all-start = ((bf16[16,16,2176]{2,1,0:T(8,128)(2,1)}), bf16[16,16,2176]{2,1,0:T(8,128)(2,1)}, u32[]{:S(2)}, u32[]{:S(2)}) async-start(bf16[16,16,2176]{2,1,0:T(8,128)(2,1)} %join.1), calls=%async_computation | async-start | bytes 2228224 | tf_op jit(solution)/shard_map/all_to_all | solution.py:374
  57.5 14.1 %collective-permute-start.9 = (bf16[128,2048]{1,0:T(8,128)(2,1)}, bf16[128,2048]{1,0:T(8,128)(2,1)S(1)}, u32[]{:S(2)}, u32[]{:S(2)}) collective-permute-start(bf16[128,2048]{1,0:T(8,128)(2,1)} %get-tuple-element.30), channel_id=1, source_target_pairs={{0,192},{64,0},{128,64},{192,128},{1,193},{65,1},{129,65},{193,129... | collective-permute-start | bytes 1572872 | tf_op jit(solution)/shard_map/ppermute | solution.py:15
  58.0 17.1 %collective-permute-start.8 = (bf16[128,2048]{1,0:T(8,128)(2,1)}, bf16[128,2048]{1,0:T(8,128)(2,1)S(1)}, u32[]{:S(2)}, u32[]{:S(2)}) collective-permute-start(bf16[128,2048]{1,0:T(8,128)(2,1)} %get-tuple-element.30), channel_id=1, source_target_pairs={{0,64},{64,128},{128,192},{192,0},{1,65},{65,129},{129,193},{193,1... | collective-permute-start | bytes 1572872 | tf_op jit(solution)/shard_map/ppermute | solution.py:15
  59.6 19.9 %collective-permute-start.16 = (bf16[128,2048]{1,0:T(8,128)(2,1)}, bf16[128,2048]{1,0:T(8,128)(2,1)S(1)}, u32[]{:S(2)}, u32[]{:S(2)}) collective-permute-start(bf16[128,2048]{1,0:T(8,128)(2,1)} %collective-permute-done.10.refs_2_), channel_id=1, source_target_pairs={{0,2},{2,0},{4,6},{6,4},{8,10},{10,8},{12,14},{14,12},{16,18},{18,... | collective-permute-start | bytes 1572872 | tf_op jit(solution)/shard_map/ppermute | solution.py:27
  59.6 23.3 %collective-permute-start.13 = (bf16[128,2048]{1,0:T(8,128)(2,1)}, bf16[128,2048]{1,0:T(8,128)(2,1)S(1)}, u32[]{:S(2)}, u32[]{:S(2)}) collective-permute-start(bf16[128,2048]{1,0:T(8,128)(2,1)} %collective-permute-done.10.refs_2_), channel_id=1, source_target_pairs={{0,32},{2,34},{4,36},{6,38},{8,40},{10,42},{12,44},{14,46},{16,48}... | collective-permute-start | bytes 1572872 | tf_op jit(solution)/shard_map/ppermute | solution.py:27
  61.4 13.7 %collective-permute-start.22 = (f32[1,1792]{1,0:T(1,128)S(1)}, f32[1,1792]{1,0:T(1,128)S(1)}, u32[]{:S(2)}, u32[]{:S(2)}) collective-permute-start(f32[1,1792]{1,0:T(1,128)S(1)} %add.18.mine.refs_16_), channel_id=1, source_target_pairs={{0,192},{64,0},{128,64},{192,128},{1,193},{65,1},{129,65},{193,129... | collective-permute-start | bytes 21512 | tf_op jit(solution)/shard_map/ppermute | solution.py:15
  71.6 5.1 %collective-permute-start.21 = (f32[1,1792]{1,0:T(1,128)S(1)}, f32[1,1792]{1,0:T(1,128)S(1)}, u32[]{:S(2)}, u32[]{:S(2)}) collective-permute-start(f32[1,1792]{1,0:T(1,128)S(1)} %add.18.mine.refs_16_), channel_id=1, source_target_pairs={{0,128},{64,192},{128,0},{192,64},{1,129},{65,193},{129,1},{193,65... | collective-permute-start | bytes 21512 | tf_op jit(solution)/shard_map/ppermute | solution.py:15
  75.1 4.4 %collective-permute-start.20 = (f32[1,1792]{1,0:T(1,128)S(1)}, f32[1,1792]{1,0:T(1,128)S(1)}, u32[]{:S(2)}, u32[]{:S(2)}) collective-permute-start(f32[1,1792]{1,0:T(1,128)S(1)} %add.18.mine.refs_16_), channel_id=1, source_target_pairs={{0,64},{64,128},{128,192},{192,0},{1,65},{65,129},{129,193},{193,1... | collective-permute-start | bytes 21512 | tf_op jit(solution)/shard_map/ppermute | solution.py:15
  75.1 7.8 %collective-permute-start.15 = (bf16[128,2048]{1,0:T(8,128)(2,1)S(1)}, bf16[128,2048]{1,0:T(8,128)(2,1)S(1)}, u32[]{:S(2)}, u32[]{:S(2)}) collective-permute-start(bf16[128,2048]{1,0:T(8,128)(2,1)S(1)} %collective-permute-done.9.refs_1_), channel_id=1, source_target_pairs={{0,2},{2,0},{4,6},{6,4},{8,10},{10,8},{12,14},{14,12},{16,18},{18,... | collective-permute-start | bytes 1572872 | tf_op jit(solution)/shard_map/ppermute | solution.py:27
  76.7 18.4 %collective-permute-start.12 = (bf16[128,2048]{1,0:T(8,128)(2,1)S(1)}, bf16[128,2048]{1,0:T(8,128)(2,1)S(1)}, u32[]{:S(2)}, u32[]{:S(2)}) collective-permute-start(bf16[128,2048]{1,0:T(8,128)(2,1)S(1)} %collective-permute-done.9.refs_1_), channel_id=1, source_target_pairs={{0,28},{2,30},{4,0},{6,2},{8,4},{10,6},{12,8},{14,10},{16,12},{18,... | collective-permute-start | bytes 1572872 | tf_op jit(solution)/shard_map/ppermute | solution.py:27
  79.5 16.1 %collective-permute-start.14 = (bf16[128,2048]{1,0:T(8,128)(2,1)S(1)}, bf16[128,2048]{1,0:T(8,128)(2,1)S(1)}, u32[]{:S(2)}, u32[]{:S(2)}) collective-permute-start(bf16[128,2048]{1,0:T(8,128)(2,1)S(1)} %collective-permute-done.8.refs_0_), channel_id=1, source_target_pairs={{0,2},{2,0},{4,6},{6,4},{8,10},{10,8},{12,14},{14,12},{16,18},{18,... | collective-permute-start | bytes 1572872 | tf_op jit(solution)/shard_map/ppermute | solution.py:27
  79.5 17.7 %collective-permute-start.11 = (bf16[128,2048]{1,0:T(8,128)(2,1)S(1)}, bf16[128,2048]{1,0:T(8,128)(2,1)S(1)}, u32[]{:S(2)}, u32[]{:S(2)}) collective-permute-start(bf16[128,2048]{1,0:T(8,128)(2,1)S(1)} %collective-permute-done.8.refs_0_), channel_id=1, source_target_pairs={{0,4},{2,6},{4,8},{6,10},{8,12},{10,14},{12,16},{14,18},{16,20},{1... | collective-permute-start | bytes 1572872 | tf_op jit(solution)/shard_map/ppermute | solution.py:27
  82.9 14.3 %collective-permute-start.19 = (bf16[128,2048]{1,0:T(8,128)(2,1)S(1)}, bf16[128,2048]{1,0:T(8,128)(2,1)S(1)}, u32[]{:S(2)}, u32[]{:S(2)}) collective-permute-start(bf16[128,2048]{1,0:T(8,128)(2,1)S(1)} %collective-permute-done.13.refs_5_), channel_id=1, source_target_pairs={{0,2},{2,0},{4,6},{6,4},{8,10},{10,8},{12,14},{14,12},{16,18},{18,... | collective-permute-start | bytes 1572872 | tf_op jit(solution)/shard_map/ppermute | solution.py:27
  82.9 22.2 %collective-permute-start.7 = (bf16[768,512]{1,0:T(8,128)(2,1)}, bf16[768,512]{1,0:T(8,128)(2,1)S(1)}, u32[]{:S(2)}, u32[]{:S(2)}) collective-permute-start(bf16[768,512]{1,0:T(8,128)(2,1)} %copy-done), channel_id=1, source_target_pairs={{0,128},{64,192},{128,0},{192,64},{1,129},{65,193},{129,1},{193,65... | collective-permute-start | bytes 2359304 | tf_op jit(solution)/shard_map/ppermute | solution.py:15
  95.2 26.5 %collective-permute-start.6 = (bf16[768,512]{1,0:T(8,128)(2,1)}, bf16[768,512]{1,0:T(8,128)(2,1)S(1)}, u32[]{:S(2)}, u32[]{:S(2)}) collective-permute-start(bf16[768,512]{1,0:T(8,128)(2,1)} %copy-done), channel_id=1, source_target_pairs={{0,192},{64,0},{128,64},{192,128},{1,193},{65,1},{129,65},{193,129... | collective-permute-start | bytes 2359304 | tf_op jit(solution)/shard_map/ppermute | solution.py:15
  95.6 26.0 %collective-permute-start.5 = (bf16[768,512]{1,0:T(8,128)(2,1)}, bf16[768,512]{1,0:T(8,128)(2,1)S(1)}, u32[]{:S(2)}, u32[]{:S(2)}) collective-permute-start(bf16[768,512]{1,0:T(8,128)(2,1)} %copy-done), channel_id=1, source_target_pairs={{0,64},{64,128},{128,192},{192,0},{1,65},{65,129},{129,193},{193,1... | collective-permute-start | bytes 2359304 | tf_op jit(solution)/shard_map/ppermute | solution.py:15
  97.2 5.5 %collective-permute-start.18 = (bf16[128,2048]{1,0:T(8,128)(2,1)S(1)}, bf16[128,2048]{1,0:T(8,128)(2,1)S(1)}, u32[]{:S(2)}, u32[]{:S(2)}) collective-permute-start(bf16[128,2048]{1,0:T(8,128)(2,1)S(1)} %collective-permute-done.12.refs_4_), channel_id=1, source_target_pairs={{0,2},{2,0},{4,6},{6,4},{8,10},{10,8},{12,14},{14,12},{16,18},{18,... | collective-permute-start | bytes 1572872 | tf_op jit(solution)/shard_map/ppermute | solution.py:27
  97.2 5.5 %collective-permute-start.17 = (bf16[128,2048]{1,0:T(8,128)(2,1)S(1)}, bf16[128,2048]{1,0:T(8,128)(2,1)S(1)}, u32[]{:S(2)}, u32[]{:S(2)}) collective-permute-start(bf16[128,2048]{1,0:T(8,128)(2,1)S(1)} %collective-permute-done.11.refs_3_), channel_id=1, source_target_pairs={{0,2},{2,0},{4,6},{6,4},{8,10},{10,8},{12,14},{14,12},{16,18},{18,... | collective-permute-start | bytes 1572872 | tf_op jit(solution)/shard_map/ppermute | solution.py:27
  (2 other events, 2.0 us)
